TPU v7x, 32 devices: a whole 2x2x4 slice. The times are simulated.
32 devices in a mesh: section: 2 (over core), tile: 4 (over z), mem: 4 (over y, x).
Axes of the slice: x: 2, y: 2, z: 4, core: 2. Of those that a mesh axis runs over, the one named last changes fastest.
Arguments:
- state: float32 [32, 16, 64, 128], P(('section', 'mem'), None, 'tile'), may hold values from -6 to 6
- speed_x: float32 [16, 64, 128], P(None, 'tile'), may hold values from -0.35 to 0.35
- speed_y: float32 [16, 64, 128], P(None, 'tile'), may hold values from -0.35 to 0.35
- diffuse: float32 [64, 128], P('tile'), may hold values from 0.02 to 0.07
- obs_cell: int32 [4096], P('tile'), may hold values from 0 to 32767, as said below
- obs_value: float32 [4096], P('tile'), may hold values from -6 to 6
- obs_errinv: float32 [4096], P('tile'), may hold values from 0.05 to 0.5
- obs_list: int32 [32, 64, 256], P('tile'), may hold values from 0 to 3071, as said below
- obs_count: int32 [32, 64], P('tile'), may hold values from 1 to 256, as said below
Outputs:
- analysis: float32 [32, 16, 64, 128], P(('section', 'mem'), None, 'tile')
Inputs may be any that keep to these rules, and one draw needn't show every extreme that they name: `obs_cell`: level * 16 * 128 + x * 128 + y of the observation inside its tile. `obs_list`: each row holds 256 different window indices k * 1024 + i, meaning observation i of the tile k - 1 places after the domain's tile; they list window columns nearest first by horizontal distance to the domain's centre; columns beyond 4 * 4 cells and columns outside the grid count as equally far, and ties go by increasing window index, so list tails near the grid's ends may name columns outside it. Only the first obs_count slots of a domain's list are used; away from a few domains, obs_count does not exceed the number of window observations within 2.5 * 4 cells of the centre.
All inputs are finite; a program needn't handle non-finite values.
Results may differ from a plain program's by a relative error of at most 0.0003.
Values sent between devices are 32-bit elements; how exact they have to be, the bound alone decides.
No kernel may reach another device: no remote copies, remote signals or barrier semaphores. Data moves between devices by JAX's collectives and lax.ppermute only.
A program may use at most 64 MiB of HBM per device.

v0:
```python
import functools

import jax
import jax.numpy as jnp
from jax import lax
from jax.experimental import pallas as pl
from jax.experimental.pallas import tpu as pltpu
from jax.sharding import PartitionSpec as P

STEPS = 4
DB = 2
LOC = 4
LANES = 128
SUB = 8
LEVELS_AT_ONCE = 4
GROUP = ("section", "mem")
F32 = jnp.float32
BF16 = jnp.bfloat16
VMEM_LIMIT = 24 * 2**20


CENTRE, PARITY, SECTION, MEM, HAS_A, HAS_B, TILE_X = range(7)


def call(kernel, outs, place, *args, scratch=(), inputs=pltpu.VMEM):
    vmem = pl.BlockSpec(memory_space=pltpu.VMEM)
    outs = [pltpu.VMEM(shape, dtype) for shape, dtype in outs]
    return pl.pallas_call(
        kernel,
        in_specs=[pl.BlockSpec(memory_space=pltpu.SMEM)] + [vmem] * len(args),
        out_specs=[vmem] * len(outs),
        out_shape=outs,
        scratch_shapes=list(scratch),
        compiler_params=pltpu.CompilerParams(vmem_limit_bytes=VMEM_LIMIT),
    )(place, *[pltpu.with_memory_space_constraint(a, inputs) for a in args])


def split_2(value):
    high = value.astype(BF16)
    return high, (value - high.astype(F32)).astype(BF16)


def pack_kernel(
    place_ref, state_ref, sx_ref, sy_ref, diff_ref, cell_ref, value_ref, err_ref, a_ref, b_ref, info_ref
):
    fields, width_x, width_y = state_ref.shape
    levels = sx_ref.shape[0]
    even = place_ref[PARITY] == 0
    cell = cell_ref[...]
    row = cell // width_y
    rows = cell.shape[0]
    info_ref[0:rows, :] = (place_ref[TILE_X] + row % width_x).astype(F32)
    info_ref[rows : 2 * rows, :] = (cell - row * width_y).astype(F32)
    info_ref[2 * rows : 3 * rows, :] = value_ref[...]
    info_ref[3 * rows : 4 * rows, :] = err_ref[...]
    at = lax.broadcasted_iota(jnp.int32, (STEPS, width_y), 0)

    def put(slot, values):
        low, high = values[:STEPS, :], values[width_x - STEPS :, :]
        extra = slot - fields
        if 0 <= extra < 4 * rows:
            line = info_ref[extra : extra + 1, :]
            low = jnp.where(at == STEPS - 1, line, low)
            high = jnp.where(at == 0, line, high)
        a_ref[slot] = jnp.where(even, high, low)
        b_ref[slot] = jnp.where(even, low, high)

    for i in range(fields):
        put(i, state_ref[i])
    for i in range(levels):
        put(fields + i, sx_ref[i])
        put(fields + levels + i, sy_ref[i])
    put(fields + 2 * levels, diff_ref[...])


def pack(place, state, speed_x, speed_y, diffuse, obs_cell, obs_value, obs_errinv):
    memb_dev, levels, width_x, width_y = state.shape
    fields = memb_dev * levels
    chunks = obs_cell.shape[0] // LANES
    slots = fields + 2 * levels + 1
    assert 4 * chunks <= 2 * levels + 1 and width_y == LANES
    return call(
        pack_kernel,
        [((slots, STEPS, width_y), F32), ((slots, STEPS, width_y), F32), ((4 * chunks, LANES), F32)],
        place,
        state.reshape(fields, width_x, width_y),
        speed_x,
        speed_y,
        diffuse,
        obs_cell.reshape(chunks, LANES),
        obs_value.reshape(chunks, LANES),
        obs_errinv.reshape(chunks, LANES),
        inputs=pltpu.HBM,
    )


def forecast_kernel(
    share,
    mems,
    place_ref,
    state_ref,
    a_ref,
    b_ref,
    sx_ref,
    sy_ref,
    diff_ref,
    cell_ref,
    keep_ref,
    send_ref,
    obs_ref,
    all_ref,
):
    fields, width_x, width_y = state_ref.shape
    levels = sx_ref.shape[0]
    memb_dev = fields // levels
    wide = width_x + 2 * STEPS
    even = place_ref[PARITY] == 0

    def ring(slot, own):
        first, second = a_ref[slot], b_ref[slot]
        above, below = jnp.where(even, first, second), jnp.where(even, second, first)
        return jnp.concatenate([own, above, below], axis=0)

    lane = lax.broadcasted_iota(jnp.int32, (wide, width_y), 1)
    diff = ring(fields + 2 * levels, diff_ref[...])
    at_once = LEVELS_AT_ONCE if levels % LEVELS_AT_ONCE == 0 else 1

    @pl.loop(0, levels // at_once)
    def _(block):
        coefs, fields_q = [], []
        for i in range(at_once):
            level = block * at_once + i
            sx = ring(fields + level, sx_ref[level])
            sy = ring(fields + levels + level, sy_ref[level])
            from_low = jnp.maximum(sx, 0.0) + diff
            from_high = diff - jnp.minimum(sx, 0.0)
            y_low = jnp.maximum(sy, 0.0) + diff
            y_high = diff - jnp.minimum(sy, 0.0)
            keep = 1.0 - (from_low + from_high + y_low + y_high)
            y_low = jnp.where(lane == 0, 0.0, y_low)
            y_high = jnp.where(lane == width_y - 1, 0.0, y_high)
            coefs.append((keep, from_low, from_high, y_low, y_high))
            fields_q.append(
                [ring(m * levels + level, state_ref[m * levels + level]) for m in range(memb_dev)]
            )
        for _ in range(STEPS):
            for i in range(at_once):
                keep, from_low, from_high, y_low, y_high = coefs[i]
                for member in range(memb_dev):
                    q = fields_q[i][member]
                    fields_q[i][member] = (
                        keep * q
                        + from_low * pltpu.roll(q, 1, 0)
                        + from_high * pltpu.roll(q, wide - 1, 0)
                        + y_low * pltpu.roll(q, 1, 1)
                        + y_high * pltpu.roll(q, width_y - 1, 1)
                    )
        for i in range(at_once):
            for member in range(memb_dev):
                at = pl.ds(pl.multiple_of((block * at_once + i) * width_x, SUB), width_x)
                all_ref[member, at, :] = fields_q[i][member][:width_x, :]

    for k in range(mems):
        for slot, part_ref in enumerate((keep_ref, send_ref)):
            group = (place_ref[SECTION] ^ slot) * mems + (place_ref[MEM] ^ k)
            for member in range(memb_dev):
                for row in range(share):
                    part_ref[k, member, pl.ds(row * levels, levels), :] = all_ref[
                        member, pl.ds(group * share + row, levels, stride=width_x), :
                    ]

    cell = cell_ref[...]
    obs = cell.shape[1]
    cell_row = cell // width_y
    cell_y = cell - cell_row * width_y
    rows = levels * width_x
    pick = (lax.broadcasted_iota(jnp.int32, (rows, obs), 0) == cell_row).astype(F32).astype(BF16)
    pick_y = lax.broadcasted_iota(jnp.int32, (width_y, obs), 0) == cell_y
    dims = (((0,), (0,)), ((), ()))
    for member in range(memb_dev):
        high, low = split_2(all_ref[member])
        found = lax.dot_general(high, pick, dims, preferred_element_type=F32)
        found = found + lax.dot_general(low, pick, dims, preferred_element_type=F32)
        obs_ref[pl.ds(member, 1), :] = jnp.sum(jnp.where(pick_y, found, 0.0), axis=0, keepdims=True)


def forecast(place, state, a, b, speed_x, speed_y, diffuse, obs_cell, share, mems):
    memb_dev, levels, width_x, width_y = state.shape
    fields = memb_dev * levels
    return call(
        functools.partial(forecast_kernel, share, mems),
        [((mems, memb_dev, share * levels, width_y), F32)] * 2 + [((memb_dev, obs_cell.shape[0]), F32)],
        place,
        state.reshape(fields, width_x, width_y),
        a,
        b,
        speed_x,
        speed_y,
        diffuse,
        obs_cell.reshape(1, -1),
        scratch=[
            pltpu.VMEM((memb_dev, levels * width_x, width_y), F32),
        ],
    )


def join_kernel(place_ref, keep_ref, other_ref, *out_refs):
    for k, out_ref in enumerate(out_refs):
        out_ref[0] = keep_ref[k + 1]
        out_ref[1] = other_ref[k + 1]


def join(place, keep, other):
    mems, *rest = keep.shape
    return call(join_kernel, [((2, *rest), F32)] * (mems - 1), place, keep, other)


def info_reader(place_ref, ref, fields, first):
    if fields is None:
        return lambda row: ref[row : row + 1, :]
    above = (place_ref[PARITY] == 0) == first

    def read(row):
        return jnp.where(above, ref[fields + row, STEPS - 1 :, :], ref[fields + row, 0:1, :])

    return read


def weight_kernel(fields, place_ref, list_ref, count_ref, own_ref, a_ref, b_ref, weight_ref):
    domains, slots = list_ref.shape
    chunks = own_ref.shape[0] // 4
    obs = chunks * LANES
    limit = float((8 * LOC) ** 2)
    slot = lax.broadcasted_iota(jnp.int32, (domains, slots), 1)
    last = jnp.sum(
        jnp.where(slot == count_ref[...] - 1, list_ref[...], 0).astype(F32), axis=1, keepdims=True
    )
    centre_x = place_ref[CENTRE].astype(F32)
    centre_y = lax.broadcasted_iota(jnp.int32, (domains, 1), 0).astype(F32) * (2.0 * DB) + (DB - 1.0)
    parity = place_ref[PARITY]
    sources = (
        (info_reader(place_ref, own_ref, None, None), 1, None),
        (info_reader(place_ref, a_ref, fields, True), 2 - 2 * parity, place_ref[HAS_A]),
        (info_reader(place_ref, b_ref, fields, False), 2 * parity, place_ref[HAS_B]),
    )

    def chunk_of(source, chunk):
        read, tile_slot, present = source
        delta_x = 2.0 * read(chunk) - centre_x
        delta_y = 2.0 * read(chunks + chunk) - centre_y
        dist = delta_x * delta_x + delta_y * delta_y
        inside = jnp.minimum(dist, limit)
        if present is not None:
            inside = jnp.where(present > 0, inside, limit)
        first = jnp.asarray(tile_slot * obs + chunk * LANES, jnp.int32)
        column = (lax.broadcasted_iota(jnp.int32, (1, LANES), 1) + first).astype(F32)
        return dist, inside * float(3 * obs) + column, column

    found = jnp.zeros((domains, LANES), F32)
    for source in sources:
        for chunk in range(chunks):
            _, score, column = chunk_of(source, chunk)
            found = found + jnp.where(column == last, score, 0.0)
    bound = jnp.sum(found, axis=1, keepdims=True)
    for n, source in enumerate(sources):
        for chunk in range(chunks):
            dist, score, _ = chunk_of(source, chunk)
            weight = source[0](3 * chunks + chunk) * jnp.exp(dist * (-1.0 / (8.0 * LOC * LOC)))
            high, low = split_2(jnp.where(score <= bound, weight, 0.0))
            at = pl.ds(n * obs + chunk * LANES, LANES)
            weight_ref[0:domains, at] = high
            weight_ref[domains : 2 * domains, at] = low


def weights(place, lists, counts, own, a, b, fields):
    domains = lists.shape[0]
    columns = 3 * (own.shape[0] // 4) * LANES
    kernel = functools.partial(weight_kernel, fields)
    return call(kernel, [((2 * domains, columns), BF16)], place, lists, counts, own, a, b)[0]


def pair_rows(members):
    starts = [SUB * (k // SUB) for k in range(members)]
    offsets, total = [], 0
    for start in starts:
        offsets.append(total)
        total += members - start
    return starts, offsets, total


def gram_of(place_ref, ens_ref, read, weight, y_ref, zh_ref, zl_ref):
    members, obs = y_ref.shape
    chunks = obs // LANES
    mems, _, memb_dev, _ = ens_ref.shape
    starts, offsets, total = pair_rows(members)
    for section in range(2):
        for mem in range(mems):
            rows = ens_ref[place_ref[MEM] ^ mem, place_ref[SECTION] ^ section]
            y_ref[pl.ds((section * mems + mem) * memb_dev, memb_dev), :] = rows
    ens = y_ref[...]
    ens_mean = jnp.mean(ens, axis=0, keepdims=True)
    y = ens - ens_mean
    y_ref[...] = y
    for k in range(0, members, 2):
        tail = y[starts[k] :, :]
        both = jnp.concatenate([tail * y_ref[k : k + 1, :], tail * y_ref[k + 1 : k + 2, :]], axis=0)
        high, low = split_2(both)
        zh_ref[pl.ds(offsets[k], both.shape[0]), :] = high
        zl_ref[pl.ds(offsets[k], both.shape[0]), :] = low
    value = jnp.concatenate([read(2 * chunks + c) for c in range(chunks)], axis=1)
    high, low = split_2(y * (value - ens_mean))
    zh_ref[pl.ds(total, members), :] = high
    zl_ref[pl.ds(total, members), :] = low
    dims = (((1,), (1,)), ((), ()))
    part = lax.dot_general(zh_ref[...], weight, dims, preferred_element_type=F32)
    return part + lax.dot_general(zl_ref[...], weight, dims, preferred_element_type=F32)


def gram_scratch(members, obs):
    _, _, total = pair_rows(members)
    return [
        pltpu.VMEM((members, obs), F32),
        pltpu.VMEM((total + members, obs), BF16),
        pltpu.VMEM((total + members, obs), BF16),
    ]


def own_gram_kernel(place_ref, own_ref, info_ref, weight_ref, out_ref, y_ref, zh_ref, zl_ref):
    read = info_reader(place_ref, info_ref, None, None)
    weight = weight_ref[:, 0 : y_ref.shape[1]]
    out_ref[...] = gram_of(place_ref, own_ref, read, weight, y_ref, zh_ref, zl_ref)


def ensemble(gathered):
    mems, sections, memb_dev, obs = gathered.shape
    return mems * sections * memb_dev, obs


def own_gram(place, own, info, weight):
    members, obs = ensemble(own)
    _, _, total = pair_rows(members)
    return call(
        own_gram_kernel,
        [((total + members, weight.shape[0]), F32)],
        place,
        own,
        info,
        weight,
        scratch=gram_scratch(members, obs),
    )[0]


def anomalies(place_ref, keep_ref, other_ref, near_refs, anomaly_ref, base_ref):
    members, rows, _ = anomaly_ref.shape
    mems = len(near_refs) + 1
    memb_dev = members // (2 * mems)

    def field_of(other, k, i, at):
        if k:
            return near_refs[k - 1][other, i, at, :]
        return other_ref[0, i, at, :] if other else keep_ref[0, i, at, :]

    for block in range(rows // SUB):
        at = pl.ds(block * SUB, SUB)
        fields = [
            (other, k, i, field_of(other, k, i, at))
            for other in range(2)
            for k in range(mems)
            for i in range(memb_dev)
        ]
        mean = sum(field for *_, field in fields) * (1.0 / members)
        base_ref[at, :] = mean
        for other, k, i, field in fields:
            member = ((place_ref[SECTION] ^ other) * mems + (place_ref[MEM] ^ k)) * memb_dev + i
            anomaly_ref[member, at, :] = field - mean


def transform_kernel(mems, fields, place_ref, part_ref, za_ref, zb_ref, a_ref, b_ref, weight_ref, *refs):
    keep_ref, other_ref, near_refs, refs = refs[0], refs[1], refs[2 : mems + 1], refs[mems + 1 :]
    inv_ref, anomaly_ref, base_ref, y_ref, zh_ref, zl_ref, gram_ref, low_ref, s_ref = refs
    obs = y_ref.shape[1]
    members = y_ref.shape[0]
    starts, offsets, total = pair_rows(members)
    sums = part_ref[...]
    for n, (near_ref, info_ref) in enumerate(((za_ref, a_ref), (zb_ref, b_ref))):
        read = info_reader(place_ref, info_ref, fields, n == 0)
        weight = weight_ref[:, pl.ds((n + 1) * obs, obs)]
        sums = sums + gram_of(place_ref, near_ref, read, weight, y_ref, zh_ref, zl_ref)
    anomalies(place_ref, keep_ref, other_ref, near_refs, anomaly_ref, base_ref)

    width = sums.shape[1]
    domain = lax.broadcasted_iota(jnp.int32, (width, LANES), 0) % (width // 2)
    column = lax.broadcasted_iota(jnp.int32, (width, LANES), 1) // DB
    spread = (domain == column).astype(F32).astype(BF16)
    high, low = split_2(sums)
    rest = (sums - high.astype(F32) - low.astype(F32)).astype(BF16)
    gram = jnp.dot(high, spread, preferred_element_type=F32)
    gram = gram + jnp.dot(low, spread, preferred_element_type=F32)
    gram = gram + jnp.dot(rest, spread, preferred_element_type=F32)
    gram_ref[...] = gram

    sub_row = lax.broadcasted_iota(jnp.int32, (SUB, LANES), 0)

    def every(ref, row):
        return ref[pl.ds(row, SUB, stride=0), :]

    blocks = members // SUB
    inv_ref[...] = jnp.zeros(inv_ref.shape, F32)
    mean = [jnp.zeros((SUB, LANES), F32) for _ in range(blocks)]
    for k in range(members):
        own = k // SUB
        acc = [gram_ref[pl.ds(offsets[k] - starts[k] + b * SUB, SUB), :] for b in range(own, blocks)]
        acc[0] = acc[0] + jnp.where(sub_row == k % SUB, members - 1.0, 0.0)
        inv = [jnp.zeros((SUB, LANES), F32) for _ in range(own)]
        inv.append(jnp.where(sub_row == k % SUB, 1.0, 0.0))
        forced = every(gram_ref, total + k)
        for j in range(k):
            base = offsets[j] - starts[j]
            factor = every(low_ref, base + k)
            for b in range(own, blocks):
                acc[b - own] = acc[b - own] - low_ref[pl.ds(base + b * SUB, SUB), :] * factor
            for b in range(j // SUB + 1):
                inv[b] = inv[b] - inv_ref[j, pl.ds(b * SUB, SUB), :] * factor
            forced = forced - s_ref[j] * factor
        pivot = jnp.broadcast_to(acc[0][k % SUB : k % SUB + 1, :], (SUB, LANES))
        scale = lax.rsqrt(pivot)
        scale = scale * (1.5 - 0.5 * pivot * scale * scale)
        for b in range(own, blocks):
            low_ref[pl.ds(offsets[k] - starts[k] + b * SUB, SUB), :] = acc[b - own] * scale
        forced = forced * scale
        s_ref[k] = forced
        for b in range(own + 1):
            inv[b] = inv[b] * scale
            inv_ref[k, pl.ds(b * SUB, SUB), :] = inv[b]
            mean[b] = mean[b] + inv[b] * forced
    for row in range(base_ref.shape[0] // SUB):
        at = pl.ds(row * SUB, SUB)
        base = base_ref[at, :]
        for j in range(members):
            shift = jnp.broadcast_to(mean[j // SUB][j % SUB : j % SUB + 1, :], (SUB, LANES))
            base = base + anomaly_ref[j, at, :] * shift
        base_ref[at, :] = base


def transforms(place, part, near_a, near_b, a, b, weight, keep, other, near, fields):
    members, obs = ensemble(near_a)
    _, _, total = pair_rows(members)
    rows = keep.shape[2]
    return call(
        functools.partial(transform_kernel, keep.shape[0], fields),
        [
            ((members, members, LANES), F32),
            ((members, rows, LANES), F32),
            ((rows, LANES), F32),
        ],
        place,
        part,
        near_a,
        near_b,
        a,
        b,
        weight,
        keep,
        other,
        *near,
        scratch=gram_scratch(members, obs)
        + [
            pltpu.VMEM((total + members, LANES), F32),
            pltpu.VMEM((total, LANES), F32),
            pltpu.VMEM((members, SUB, LANES), F32),
        ],
    )


def apply_kernel(mems, k, place_ref, anomaly_ref, base_ref, inv_ref, *out_refs):
    members, rows, _ = anomaly_ref.shape
    memb_dev = members // (2 * mems)
    root = float(members - 1) ** 0.5
    blocks = rows // SUB
    if len(out_refs) == 1:
        out_refs = [out_refs[0].at[slot] for slot in range(2)]
    for slot in range(2):
        group = (place_ref[SECTION] ^ slot) * mems + (place_ref[MEM] ^ k)
        first = group * memb_dev
        zero = tuple(jnp.zeros((SUB, LANES), F32) for _ in range(memb_dev * blocks))

        def step(chunk, acc, first=first):
            acc = list(acc)
            for t in range(memb_dev):
                j = chunk * memb_dev + t
                fields = [anomaly_ref[j, pl.ds(b * SUB, SUB), :] for b in range(blocks)]
                for i in range(memb_dev):
                    factor = inv_ref[first + i, pl.ds(j, SUB, stride=0), :]
                    for b in range(blocks):
                        acc[i * blocks + b] = acc[i * blocks + b] + fields[b] * factor
            return tuple(acc)

        acc = lax.fori_loop(0, group + 1, step, zero)
        for i in range(memb_dev):
            for b in range(blocks):
                at = pl.ds(b * SUB, SUB)
                out_refs[slot][i, at, :] = base_ref[at, :] + root * acc[i * blocks + b]


def apply_transform(place, anomaly, base, inverse, mems, k, split):
    members, rows, width_y = anomaly.shape
    block = (members // (2 * mems), rows, width_y)
    outs = [(block, F32)] * 2 if split else [((2, *block), F32)]
    return call(functools.partial(apply_kernel, mems, k), outs, place, anomaly, base, inverse)


def unpack_kernel(share, mems, place_ref, *refs):
    near_refs, far_refs, (out_ref, all_ref, sem_ref) = refs[:mems], refs[mems : 2 * mems], refs[2 * mems :]
    memb_dev, total, _ = all_ref.shape
    levels = total // (2 * mems * share)
    width_x = total // levels
    copies = []
    for i in range(memb_dev):
        for other in range(2):
            for k in range(mems):
                group = (place_ref[SECTION] ^ other) * mems + (place_ref[MEM] ^ k)
                block_ref = (far_refs if other else near_refs)[k]
                if len(block_ref.shape) == 4:
                    block_ref = block_ref.at[other]
                for row in range(share):
                    all_ref[i, pl.ds(group * share + row, levels, stride=width_x), :] = block_ref[
                        i, pl.ds(row * levels, levels), :
                    ]
        copies.append(pltpu.make_async_copy(all_ref.at[i], out_ref.at[i], sem_ref.at[i]))
        copies[-1].start()
    for copy in copies:
        copy.wait()


def unpack(place, near, far, share, mems):
    memb_dev, rows, width_y = near[0].shape[-3:]
    vmem = pl.BlockSpec(memory_space=pltpu.VMEM)
    shape = (memb_dev, 2 * mems * rows, width_y)
    return pl.pallas_call(
        functools.partial(unpack_kernel, share, mems),
        in_specs=[pl.BlockSpec(memory_space=pltpu.SMEM)] + [vmem] * (2 * mems),
        out_specs=pl.BlockSpec(memory_space=pltpu.HBM),
        out_shape=jax.ShapeDtypeStruct(shape, F32),
        scratch_shapes=[pltpu.VMEM(shape, F32), pltpu.SemaphoreType.DMA((memb_dev,))],
        compiler_params=pltpu.CompilerParams(vmem_limit_bytes=VMEM_LIMIT),
        name="unpack",
    )(place, *[pltpu.with_memory_space_constraint(x, pltpu.VMEM) for x in (*near, *far)])


def along_tile(first, second):
    count = lax.axis_size("tile")

    def trade(value, start):
        pairs = []
        for i in range(start, count - 1, 2):
            pairs += [(i, i + 1), (i + 1, i)]
        return lax.ppermute(value, "tile", pairs)

    first = trade(first, 0)
    second = trade(second, 1)
    return first, second


def to_partner(value):
    return lax.ppermute(value, "section", [(0, 1), (1, 0)])


def over_mem(value, k):
    return lax.ppermute(value, "mem", [(i, i ^ k) for i in range(lax.axis_size("mem"))])


def across(value, k):
    size = lax.axis_size(GROUP)
    return lax.ppermute(value, GROUP, [(i, i ^ (size // 2) ^ k) for i in range(size)])


def analysis(state, speed_x, speed_y, diffuse, obs_cell, obs_value, obs_errinv, obs_list, obs_count):
    memb_dev, levels, width_x, _ = state.shape
    mems = lax.axis_size("mem")
    groups = lax.axis_size(GROUP)
    assert groups == 2 * mems and mems & (mems - 1) == 0
    tiles = lax.axis_size("tile")
    tile = lax.axis_index("tile")
    group_idx = lax.axis_index(GROUP)
    share = width_x // groups
    far = list(range(mems - 1, 0, -1))

    parity = tile % 2
    place = jnp.stack(
        [
            2 * (tile * width_x + group_idx * share) + DB - 1,
            parity,
            lax.axis_index("section"),
            lax.axis_index("mem"),
            ((parity == 1) | (tile < tiles - 1)).astype(jnp.int32),
            jnp.where(parity == 1, tile < tiles - 1, tile > 0).astype(jnp.int32),
            tile * width_x,
        ]
    ).astype(jnp.int32)

    share_d = share // DB
    lists = lax.dynamic_slice_in_dim(obs_list, group_idx * share_d, share_d, 0)
    lists = lists.reshape(-1, obs_list.shape[2])
    counts = lax.dynamic_slice_in_dim(obs_count, group_idx * share_d, share_d, 0).reshape(-1, 1)

    a, b, info = pack(place, state, speed_x, speed_y, diffuse, obs_cell, obs_value, obs_errinv)
    a, b = along_tile(a, b)
    keep, send, own_obs = forecast(
        place, state, a, b, speed_x, speed_y, diffuse, obs_cell, share, mems
    )

    other_obs = to_partner(own_obs)
    other = to_partner(send)
    both_obs = jnp.stack([own_obs, other_obs])
    gathered = [both_obs] + [over_mem(both_obs, k) for k in far[::-1]]
    gathered = jnp.stack(gathered)
    joined = join(place, keep, other)
    near = [over_mem(joined[k - 1], k) for k in far[::-1]]
    near_a, near_b = along_tile(gathered, gathered)
    weight = weights(place, lists, counts, info, a, b, memb_dev * levels)
    part = own_gram(place, gathered, info, weight)
    inverse, anomaly, base = transforms(
        place, part, near_a, near_b, a, b, weight, keep, other, near, memb_dev * levels
    )

    direct = None
    done, away = [None] * mems, [None] * mems
    for k in far + [0]:
        result = apply_transform(place, anomaly, base, inverse, mems, k, k == direct)
        done[k] = over_mem(result[0], k) if k else result[0]
        if k == direct:
            away[k] = across(result[1], k)
    for k in range(mems):
        if k != direct:
            away[k] = to_partner(done[k])
    return unpack(place, done, away, share, mems).reshape(state.shape)


def solution(mesh):
    placed = (
        P(GROUP, None, "tile", None),
        P(None, "tile", None),
        P(None, "tile", None),
        P("tile", None),
        P("tile"),
        P("tile"),
        P("tile"),
        P("tile", None, None),
        P("tile", None),
    )
    return jax.shard_map(
        analysis,
        mesh=mesh,
        in_specs=placed,
        out_specs=P(GROUP, None, "tile", None),
        check_vma=False,
    )
```

profile of v0, /device:TPU:0, one launch (start us, length us, event | category | flops | bytes accessed | tf_op | source)
XLA Modules:
  0.0 56.1 jit_solution(2230885234275300639)
XLA Ops:
  0.0 0.0 copy-start
  0.0 0.0 copy-start.1
  0.0 0.1 stack.63.place_ref
  0.1 0.0 copy-start.2
  0.1 0.0 copy-start.3
  0.1 0.0 copy-start.4
  0.1 1.3 %shard_map.91 = (f32[97,4,128]{2,1,0:T(4,128)S(1)}, f32[97,4,128]{2,1,0:T(4,128)S(1)}, f32[32,128]{1,0:T(8,128)S(1)}) custom-call(s32[7]{0:T(128)S(1)} %stack.63.place_ref, f32[64,16,128]{2,1,0:T(8,128)} %bitcast.24, f32[16,16,128]{2,1,0:T(8,128)} %sx_ref.3, f32[16,16,128]{2,1,0:T(8,128)} %sy_ref.3, f32[16,128]{1,0:T(8,128)} %diff_ref.3, s32[8,128]{1,0:T(8,128)} %bitcast.26, ...), custom_call_target="tpu_custom_call" | custom-call | tf_op jit(solution)/shard_map/pallas_call | solution.py:28
  1.4 0.0 copy-start.5
  1.5 3.1 %collective-permute-start = (f32[97,4,128]{2,1,0:T(4,128)S(1)}, f32[97,4,128]{2,1,0:T(4,128)S(1)}, u32[]{:S(2)}, u32[]{:S(2)}) collective-permute-start(f32[97,4,128]{2,1,0:T(4,128)S(1)} %get-tuple-element.17), channel_id=1, source_target_pairs={{0,4},{4,0},{8,12},{12,8},{1,5},{5,1},{9,13},{13,9},{2,6},{6,2},{1... | collective-permute-start | bytes 595976 | tf_op jit(solution)/shard_map/ppermute | solution.py:557
  4.6 0.7 %collective-permute-start.1 = (f32[97,4,128]{2,1,0:T(4,128)S(1)}, f32[97,4,128]{2,1,0:T(4,128)S(1)}, u32[]{:S(2)}, u32[]{:S(2)}) collective-permute-start(f32[97,4,128]{2,1,0:T(4,128)S(1)} %get-tuple-element.18), channel_id=1, source_target_pairs={{4,8},{8,4},{5,9},{9,5},{6,10},{10,6},{7,11},{11,7},{20,24},{24,20... | collective-permute-start | bytes 595976 | tf_op jit(solution)/shard_map/ppermute | solution.py:557
  5.2 4.3 %collective-permute-done.a_ref = f32[97,4,128]{2,1,0:T(4,128)S(1)} collective-permute-done((f32[97,4,128]{2,1,0:T(4,128)S(1)}, f32[97,4,128]{2,1,0:T(4,128)S(1)}, u32[]{:S(2)}, u32[]{:S(2)}) %collective-permute-start) | collective-permute-done | bytes 198688 | tf_op jit(solution)/shard_map/ppermute | solution.py:557
  9.5 0.0 collective-permute-done.1.b_ref
  9.5 0.0 copy-done.1
  9.5 0.0 copy-done.2
  9.5 0.0 copy-done.3
  9.5 0.0 copy-done.4
  9.6 0.0 copy-done.5
  9.6 3.5 %shard_map.92 = (f32[4,4,32,128]{3,2,1,0:T(8,128)S(1)}, f32[4,4,32,128]{3,2,1,0:T(8,128)S(1)}, f32[4,1024]{1,0:T(4,128)S(1)}) custom-call(s32[7]{0:T(128)S(1)} %stack.63.place_ref, f32[64,16,128]{2,1,0:T(8,128)S(1)} %bitcast.25, f32[97,4,128]{2,1,0:T(4,128)S(1)} %collective-permute-done.a_ref, f32[97,4,128]{2,1,0:T(4,128)S(1)} %collective-permute-done.1.b_ref, ...), custom_call_target="tpu_custom_call" | custom-call | tf_op jit(solution)/shard_map/pallas_call | solution.py:28
  13.0 0.1 collective-permute-start.2
  13.1 0.5 collective-permute-start.8
  13.6 0.7 %collective-permute-done.2 = f32[4,1024]{1,0:T(4,128)S(1)} collective-permute-done((f32[4,1024]{1,0:T(4,128)S(1)}, f32[4,1024]{1,0:T(4,128)S(1)}, u32[]{:S(2)}, u32[]{:S(2)}) %collective-permute-start.2) | collective-permute-done | bytes 16416 | tf_op jit(solution)/shard_map/ppermute | solution.py:565
  14.3 1.8 %collective-permute-start.4 = (f32[2,4,1024]{2,1,0:T(4,128)S(1)}, f32[2,4,1024]{2,1,0:T(4,128)S(1)}, u32[]{:S(2)}, u32[]{:S(2)}) collective-permute-start(f32[2,4,1024]{2,1,0:T(4,128)S(1)} %get-tuple-element.30), channel_id=1, source_target_pairs={{0,2},{1,3},{2,0},{3,1},{4,6},{5,7},{6,4},{7,5},{8,10},{9,11},{10,... | collective-permute-start | bytes 98312 | tf_op jit(solution)/shard_map/ppermute | solution.py:569
  16.0 1.5 %collective-permute-start.3 = (f32[2,4,1024]{2,1,0:T(4,128)S(1)}, f32[2,4,1024]{2,1,0:T(4,128)S(1)}, u32[]{:S(2)}, u32[]{:S(2)}) collective-permute-start(f32[2,4,1024]{2,1,0:T(4,128)S(1)} %get-tuple-element.30), channel_id=1, source_target_pairs={{0,1},{1,0},{2,3},{3,2},{4,5},{5,4},{6,7},{7,6},{8,9},{9,8},{10,11... | collective-permute-start | bytes 98312 | tf_op jit(solution)/shard_map/ppermute | solution.py:569
  17.5 0.3 collective-permute-start.5
  17.8 0.4 collective-permute-done.4
  18.3 2.0 %collective-permute-done.3 = f32[2,4,1024]{2,1,0:T(4,128)S(1)} collective-permute-done((f32[2,4,1024]{2,1,0:T(4,128)S(1)}, f32[2,4,1024]{2,1,0:T(4,128)S(1)}, u32[]{:S(2)}, u32[]{:S(2)}) %collective-permute-start.3) | collective-permute-done | bytes 32800 | tf_op jit(solution)/shard_map/ppermute | solution.py:569
  20.2 2.1 %collective-permute-done.5 = f32[2,4,1024]{2,1,0:T(4,128)S(1)} collective-permute-done((f32[2,4,1024]{2,1,0:T(4,128)S(1)}, f32[2,4,1024]{2,1,0:T(4,128)S(1)}, u32[]{:S(2)}, u32[]{:S(2)}) %collective-permute-start.5) | collective-permute-done | bytes 32800 | tf_op jit(solution)/shard_map/ppermute | solution.py:569
  22.4 0.7 %collective-permute-start.7 = (f32[4,2,4,1024]{3,2,1,0:T(4,128)S(1)}, f32[4,2,4,1024]{3,2,1,0:T(4,128)S(1)}, u32[]{:S(2)}, u32[]{:S(2)}) collective-permute-start(f32[4,2,4,1024]{3,2,1,0:T(4,128)S(1)} %pad_maximum_fusion.own_ref), channel_id=1, source_target_pairs={{4,8},{8,4},{5,9},{9,5},{6,10},{10,6},{7,11},{11,7},{20,24},{24,20... | collective-permute-start | bytes 393224 | tf_op jit(solution)/shard_map/ppermute | solution.py:557
  23.1 7.6 %collective-permute-start.6 = (f32[4,2,4,1024]{3,2,1,0:T(4,128)S(1)}, f32[4,2,4,1024]{3,2,1,0:T(4,128)S(1)}, u32[]{:S(2)}, u32[]{:S(2)}) collective-permute-start(f32[4,2,4,1024]{3,2,1,0:T(4,128)S(1)} %pad_maximum_fusion.own_ref), channel_id=1, source_target_pairs={{0,4},{4,0},{8,12},{12,8},{1,5},{5,1},{9,13},{13,9},{2,6},{6,2},{1... | collective-permute-start | bytes 393224 | tf_op jit(solution)/shard_map/ppermute | solution.py:557
  30.7 0.0 collective-permute-done.8.other_ref.refs_1_
  30.7 0.6 %shard_map.95 = (f32[2,4,32,128]{3,2,1,0:T(8,128)S(1)}, f32[2,4,32,128]{3,2,1,0:T(8,128)S(1)}, f32[2,4,32,128]{3,2,1,0:T(8,128)S(1)}) custom-call(s32[7]{0:T(128)S(1)} %stack.63.place_ref, f32[4,4,32,128]{3,2,1,0:T(8,128)S(1)} %get-tuple-element.21.keep_ref.refs_0_, f32[4,4,32,128]{3,2,1,0:T(8,128)S(1)} %collective-permute-done.8.other_ref.refs_1_), custom_call_target="tpu_custom_call" | custom-call | tf_op jit(solution)/shard_map/pallas_call | solution.py:28
  31.3 0.6 %collective-permute-start.9 = (f32[2,4,32,128]{3,2,1,0:T(8,128)S(1)}, f32[2,4,32,128]{3,2,1,0:T(8,128)S(1)}, u32[]{:S(2)}, u32[]{:S(2)}) collective-permute-start(f32[2,4,32,128]{3,2,1,0:T(8,128)S(1)} %get-tuple-element.23), channel_id=1, source_target_pairs={{0,1},{1,0},{2,3},{3,2},{4,5},{5,4},{6,7},{7,6},{8,9},{9,8},{10,11... | collective-permute-start | bytes 393224 | tf_op jit(solution)/shard_map/ppermute | solution.py:569
  31.9 0.5 collective-permute-start.10
  32.4 2.4 %collective-permute-start.11 = (f32[2,4,32,128]{3,2,1,0:T(8,128)S(1)}, f32[2,4,32,128]{3,2,1,0:T(8,128)S(1)}, u32[]{:S(2)}, u32[]{:S(2)}) collective-permute-start(f32[2,4,32,128]{3,2,1,0:T(8,128)S(1)} %get-tuple-element.25), channel_id=1, source_target_pairs={{0,3},{1,2},{2,1},{3,0},{4,7},{5,6},{6,5},{7,4},{8,11},{9,10},{10,... | collective-permute-start | bytes 393224 | tf_op jit(solution)/shard_map/ppermute | solution.py:569
  34.8 0.7 %dynamic-slice_bitcast_fusion.1 = s32[64,1]{0,1:T(1,128)S(1)} fusion(s32[8,64]{1,0:T(8,128)} %param.17, s32[]{:T(128)S(6)} %select_n.17), kind=kLoop, calls=%fused_computation.3 | loop fusion | bytes 516 | tf_op jit(solution)/shard_map/reshape | solution.py:604
  35.5 0.1 copy.10.count_ref
  35.6 0.0 copy-done
  35.6 1.4 %shard_map.93.weight_ref = bf16[128,3072]{1,0:T(8,128)(2,1)S(1)} custom-call(s32[7]{0:T(128)S(1)} %stack.63.place_ref, s32[64,256]{1,0:T(8,128)S(1)} %dynamic-slice_bitcast_fusion.list_ref, s32[64,1]{1,0:T(8,128)S(1)} %copy.10.count_ref, f32[32,128]{1,0:T(8,128)S(1)} %get-tuple-element.20.own_ref.info_ref, f32[97,4,128]{2,1,0:T(4,128)S(1)} %collective-permute-done.a_ref, ...), custom_call_target="tpu_custom_call" | custom-call | tf_op jit(solution)/shard_map/pallas_call | solution.py:28
  37.0 1.4 %shard_map.94.part_ref = f32[672,128]{1,0:T(8,128)S(1)} custom-call(s32[7]{0:T(128)S(1)} %stack.63.place_ref, f32[4,2,4,1024]{3,2,1,0:T(4,128)S(1)} %pad_maximum_fusion.own_ref, f32[32,128]{1,0:T(8,128)S(1)} %get-tuple-element.20.own_ref.info_ref, bf16[128,3072]{1,0:T(8,128)(2,1)S(1)} %shard_map.93.weight_ref), custom_call_target="tpu_custom_call" | custom-call | tf_op jit(solution)/shard_map/pallas_call | solution.py:28
  38.5 0.0 collective-permute-done.7.zb_ref
  38.5 0.0 collective-permute-done.6.za_ref
  38.5 0.0 collective-permute-done.9.refs_2_
  38.5 0.0 collective-permute-done.10.refs_3_
  38.5 0.0 collective-permute-done.11.refs_4_
  38.5 3.7 %shard_map.96 = (f32[32,32,128]{2,1,0:T(8,128)S(1)}, f32[32,32,128]{2,1,0:T(8,128)S(1)}, f32[32,128]{1,0:T(8,128)S(1)}) custom-call(s32[7]{0:T(128)S(1)} %stack.63.place_ref, f32[672,128]{1,0:T(8,128)S(1)} %shard_map.94.part_ref, f32[4,2,4,1024]{3,2,1,0:T(4,128)S(1)} %collective-permute-done.6.za_ref, f32[4,2,4,1024]{3,2,1,0:T(4,128)S(1)} %collective-permute-done.7.zb_ref, ...), custom_call_target="tpu_custom_call" | custom-call | tf_op jit(solution)/shard_map/pallas_call | solution.py:28
  42.3 0.7 %shard_map.98 = f32[2,4,32,128]{3,2,1,0:T(8,128)S(1)} custom-call(s32[7]{0:T(128)S(1)} %stack.63.place_ref, f32[32,32,128]{2,1,0:T(8,128)S(1)} %get-tuple-element.26.anomaly_ref, f32[32,128]{1,0:T(8,128)S(1)} %get-tuple-element.27.base_ref, f32[32,32,128]{2,1,0:T(8,128)S(1)} %get-tuple-element.28.inv_ref), custom_call_target="tpu_custom_call" | custom-call | tf_op jit(solution)/shard_map/pallas_call | solution.py:28
  43.0 1.4 %collective-permute-start.12 = (f32[2,4,32,128]{3,2,1,0:T(8,128)S(1)}, f32[2,4,32,128]{3,2,1,0:T(8,128)S(1)}, u32[]{:S(2)}, u32[]{:S(2)}) collective-permute-start(f32[2,4,32,128]{3,2,1,0:T(8,128)S(1)} %shard_map.98), channel_id=1, source_target_pairs={{0,1},{1,0},{2,3},{3,2},{4,5},{5,4},{6,7},{7,6},{8,9},{9,8},{10,11... | collective-permute-start | bytes 393224 | tf_op jit(solution)/shard_map/ppermute | solution.py:569
  44.5 0.8 %shard_map.99 = f32[2,4,32,128]{3,2,1,0:T(8,128)S(1)} custom-call(s32[7]{0:T(128)S(1)} %stack.63.place_ref, f32[32,32,128]{2,1,0:T(8,128)S(1)} %get-tuple-element.26.anomaly_ref, f32[32,128]{1,0:T(8,128)S(1)} %get-tuple-element.27.base_ref, f32[32,32,128]{2,1,0:T(8,128)S(1)} %get-tuple-element.28.inv_ref), custom_call_target="tpu_custom_call" | custom-call | tf_op jit(solution)/shard_map/pallas_call | solution.py:28
  45.3 1.3 %collective-permute-start.13 = (f32[2,4,32,128]{3,2,1,0:T(8,128)S(1)}, f32[2,4,32,128]{3,2,1,0:T(8,128)S(1)}, u32[]{:S(2)}, u32[]{:S(2)}) collective-permute-start(f32[2,4,32,128]{3,2,1,0:T(8,128)S(1)} %shard_map.99), channel_id=1, source_target_pairs={{0,2},{1,3},{2,0},{3,1},{4,6},{5,7},{6,4},{7,5},{8,10},{9,11},{10,... | collective-permute-start | bytes 393224 | tf_op jit(solution)/shard_map/ppermute | solution.py:569
  46.6 0.8 %shard_map.100 = f32[2,4,32,128]{3,2,1,0:T(8,128)S(1)} custom-call(s32[7]{0:T(128)S(1)} %stack.63.place_ref, f32[32,32,128]{2,1,0:T(8,128)S(1)} %get-tuple-element.26.anomaly_ref, f32[32,128]{1,0:T(8,128)S(1)} %get-tuple-element.27.base_ref, f32[32,32,128]{2,1,0:T(8,128)S(1)} %get-tuple-element.28.inv_ref), custom_call_target="tpu_custom_call" | custom-call | tf_op jit(solution)/shard_map/pallas_call | solution.py:28
  47.4 0.8 %collective-permute-start.14 = (f32[2,4,32,128]{3,2,1,0:T(8,128)S(1)}, f32[2,4,32,128]{3,2,1,0:T(8,128)S(1)}, u32[]{:S(2)}, u32[]{:S(2)}) collective-permute-start(f32[2,4,32,128]{3,2,1,0:T(8,128)S(1)} %shard_map.100), channel_id=1, source_target_pairs={{0,3},{1,2},{2,1},{3,0},{4,7},{5,6},{6,5},{7,4},{8,11},{9,10},{10,... | collective-permute-start | bytes 393224 | tf_op jit(solution)/shard_map/ppermute | solution.py:569
  48.2 0.7 %shard_map.97.refs_0_ = f32[2,4,32,128]{3,2,1,0:T(8,128)S(1)} custom-call(s32[7]{0:T(128)S(1)} %stack.63.place_ref, f32[32,32,128]{2,1,0:T(8,128)S(1)} %get-tuple-element.26.anomaly_ref, f32[32,128]{1,0:T(8,128)S(1)} %get-tuple-element.27.base_ref, f32[32,32,128]{2,1,0:T(8,128)S(1)} %get-tuple-element.28.inv_ref), custom_call_target="tpu_custom_call" | custom-call | tf_op jit(solution)/shard_map/pallas_call | solution.py:28
  48.9 0.1 collective-permute-start.15
  49.0 0.2 collective-permute-done.12.refs_1_
  49.2 0.3 collective-permute-start.16
  49.5 1.4 %collective-permute-done.13.refs_2_ = f32[2,4,32,128]{3,2,1,0:T(8,128)S(1)} collective-permute-done((f32[2,4,32,128]{3,2,1,0:T(8,128)S(1)}, f32[2,4,32,128]{3,2,1,0:T(8,128)S(1)}, u32[]{:S(2)}, u32[]{:S(2)}) %collective-permute-start.13) | collective-permute-done | bytes 131104 | tf_op jit(solution)/shard_map/ppermute | solution.py:569
  50.9 0.0 collective-permute-start.17
  50.9 2.5 %collective-permute-done.14.refs_3_ = f32[2,4,32,128]{3,2,1,0:T(8,128)S(1)} collective-permute-done((f32[2,4,32,128]{3,2,1,0:T(8,128)S(1)}, f32[2,4,32,128]{3,2,1,0:T(8,128)S(1)}, u32[]{:S(2)}, u32[]{:S(2)}) %collective-permute-start.14) | collective-permute-done | bytes 131104 | tf_op jit(solution)/shard_map/ppermute | solution.py:569
  53.4 0.0 collective-permute-start.18
  53.4 0.0 collective-permute-done.15.refs_4_
  53.4 0.0 collective-permute-done.16.refs_5_
  53.4 0.0 collective-permute-done.17.refs_6_
  53.4 1.3 %collective-permute-done.18.refs_7_ = f32[2,4,32,128]{3,2,1,0:T(8,128)S(1)} collective-permute-done((f32[2,4,32,128]{3,2,1,0:T(8,128)S(1)}, f32[2,4,32,128]{3,2,1,0:T(8,128)S(1)}, u32[]{:S(2)}, u32[]{:S(2)}) %collective-permute-start.18) | collective-permute-done | bytes 131104 | tf_op jit(solution)/shard_map/ppermute | solution.py:565
  54.7 1.4 %unpack.1 = f32[4,256,128]{2,1,0:T(8,128)} custom-call(s32[7]{0:T(128)S(1)} %stack.63.place_ref, f32[2,4,32,128]{3,2,1,0:T(8,128)S(1)} %shard_map.97.refs_0_, f32[2,4,32,128]{3,2,1,0:T(8,128)S(1)} %collective-permute-done.12.refs_1_, f32[2,4,32,128]{3,2,1,0:T(8,128)S(1)} %collective-permute-done.13.refs_2_, ...), custom_call_target="tpu_custom_call" | custom-call | tf_op jit(solution)/shard_map/unpack/pallas_call | solution.py:539
  (3 shorter events, 0.1 us)
Async XLA Ops:
  0.0 35.6 %copy-start = (s32[8,64,256]{2,1,0:T(8,128)S(1)}, s32[8,64,256]{2,1,0:T(8,128)}, u32[]{:S(2)}) copy-start(s32[8,64,256]{2,1,0:T(8,128)} %param.16) | copy-start | bytes 1572868
  0.0 9.5 %copy-start.1 = (f32[4,16,16,128]{3,2,1,0:T(8,128)S(1)}, f32[4,16,16,128]{3,2,1,0:T(8,128)}, u32[]{:S(2)}) copy-start(f32[4,16,16,128]{3,2,1,0:T(8,128)} %param.9) | copy-start | bytes 1572868
  0.1 9.4 %copy-start.2 = (f32[16,16,128]{2,1,0:T(8,128)S(1)}, f32[16,16,128]{2,1,0:T(8,128)}, u32[]{:S(2)}) copy-start(f32[16,16,128]{2,1,0:T(8,128)} %sx_ref.3) | copy-start | bytes 393220
  0.1 9.4 %copy-start.3 = (f32[16,16,128]{2,1,0:T(8,128)S(1)}, f32[16,16,128]{2,1,0:T(8,128)}, u32[]{:S(2)}) copy-start(f32[16,16,128]{2,1,0:T(8,128)} %sy_ref.3) | copy-start | bytes 393220
  0.1 9.5 %copy-start.4 = (f32[16,128]{1,0:T(8,128)S(1)}, f32[16,128]{1,0:T(8,128)}, u32[]{:S(2)}) copy-start(f32[16,128]{1,0:T(8,128)} %diff_ref.3) | copy-start | bytes 24580
  1.4 8.1 %copy-start.5 = (s32[1024]{0:T(1024)S(1)}, s32[1024]{0:T(1024)}, u32[]{:S(2)}) copy-start(s32[1024]{0:T(1024)} %param.13) | copy-start | bytes 12292
  1.5 8.1 %collective-permute-start = (f32[97,4,128]{2,1,0:T(4,128)S(1)}, f32[97,4,128]{2,1,0:T(4,128)S(1)}, u32[]{:S(2)}, u32[]{:S(2)}) collective-permute-start(f32[97,4,128]{2,1,0:T(4,128)S(1)} %get-tuple-element.17), channel_id=1, source_target_pairs={{0,4},{4,0},{8,12},{12,8},{1,5},{5,1},{9,13},{13,9},{2,6},{6,2},{1... | collective-permute-start | bytes 595976 | tf_op jit(solution)/shard_map/ppermute | solution.py:557
  4.6 4.9 %collective-permute-start.1 = (f32[97,4,128]{2,1,0:T(4,128)S(1)}, f32[97,4,128]{2,1,0:T(4,128)S(1)}, u32[]{:S(2)}, u32[]{:S(2)}) collective-permute-start(f32[97,4,128]{2,1,0:T(4,128)S(1)} %get-tuple-element.18), channel_id=1, source_target_pairs={{4,8},{8,4},{5,9},{9,5},{6,10},{10,6},{7,11},{11,7},{20,24},{24,20... | collective-permute-start | bytes 595976 | tf_op jit(solution)/shard_map/ppermute | solution.py:557
  13.0 1.2 %collective-permute-start.2 = (f32[4,1024]{1,0:T(4,128)S(1)}, f32[4,1024]{1,0:T(4,128)S(1)}, u32[]{:S(2)}, u32[]{:S(2)}) collective-permute-start(f32[4,1024]{1,0:T(4,128)S(1)} %get-tuple-element.19), channel_id=1, source_target_pairs={{0,16},{16,0},{1,17},{17,1},{2,18},{18,2},{3,19},{19,3},{4,20},{20... | collective-permute-start | bytes 49160 | tf_op jit(solution)/shard_map/ppermute | solution.py:565
  13.1 17.6 %collective-permute-start.8 = (f32[4,4,32,128]{3,2,1,0:T(8,128)S(1)}, f32[4,4,32,128]{3,2,1,0:T(8,128)S(1)}, u32[]{:S(2)}, u32[]{:S(2)}) collective-permute-start(f32[4,4,32,128]{3,2,1,0:T(8,128)S(1)} %get-tuple-element.22), channel_id=1, source_target_pairs={{0,16},{16,0},{1,17},{17,1},{2,18},{18,2},{3,19},{19,3},{4,20},{20... | collective-permute-start | bytes 786440 | tf_op jit(solution)/shard_map/ppermute | solution.py:565
  14.3 4.0 %collective-permute-start.4 = (f32[2,4,1024]{2,1,0:T(4,128)S(1)}, f32[2,4,1024]{2,1,0:T(4,128)S(1)}, u32[]{:S(2)}, u32[]{:S(2)}) collective-permute-start(f32[2,4,1024]{2,1,0:T(4,128)S(1)} %get-tuple-element.30), channel_id=1, source_target_pairs={{0,2},{1,3},{2,0},{3,1},{4,6},{5,7},{6,4},{7,5},{8,10},{9,11},{10,... | collective-permute-start | bytes 98312 | tf_op jit(solution)/shard_map/ppermute | solution.py:569
  16.0 4.2 %collective-permute-start.3 = (f32[2,4,1024]{2,1,0:T(4,128)S(1)}, f32[2,4,1024]{2,1,0:T(4,128)S(1)}, u32[]{:S(2)}, u32[]{:S(2)}) collective-permute-start(f32[2,4,1024]{2,1,0:T(4,128)S(1)} %get-tuple-element.30), channel_id=1, source_target_pairs={{0,1},{1,0},{2,3},{3,2},{4,5},{5,4},{6,7},{7,6},{8,9},{9,8},{10,11... | collective-permute-start | bytes 98312 | tf_op jit(solution)/shard_map/ppermute | solution.py:569
  17.5 4.8 %collective-permute-start.5 = (f32[2,4,1024]{2,1,0:T(4,128)S(1)}, f32[2,4,1024]{2,1,0:T(4,128)S(1)}, u32[]{:S(2)}, u32[]{:S(2)}) collective-permute-start(f32[2,4,1024]{2,1,0:T(4,128)S(1)} %get-tuple-element.30), channel_id=1, source_target_pairs={{0,3},{1,2},{2,1},{3,0},{4,7},{5,6},{6,5},{7,4},{8,11},{9,10},{10,... | collective-permute-start | bytes 98312 | tf_op jit(solution)/shard_map/ppermute | solution.py:569
  22.4 16.1 %collective-permute-start.7 = (f32[4,2,4,1024]{3,2,1,0:T(4,128)S(1)}, f32[4,2,4,1024]{3,2,1,0:T(4,128)S(1)}, u32[]{:S(2)}, u32[]{:S(2)}) collective-permute-start(f32[4,2,4,1024]{3,2,1,0:T(4,128)S(1)} %pad_maximum_fusion.own_ref), channel_id=1, source_target_pairs={{4,8},{8,4},{5,9},{9,5},{6,10},{10,6},{7,11},{11,7},{20,24},{24,20... | collective-permute-start | bytes 393224 | tf_op jit(solution)/shard_map/ppermute | solution.py:557
  23.1 15.4 %collective-permute-start.6 = (f32[4,2,4,1024]{3,2,1,0:T(4,128)S(1)}, f32[4,2,4,1024]{3,2,1,0:T(4,128)S(1)}, u32[]{:S(2)}, u32[]{:S(2)}) collective-permute-start(f32[4,2,4,1024]{3,2,1,0:T(4,128)S(1)} %pad_maximum_fusion.own_ref), channel_id=1, source_target_pairs={{0,4},{4,0},{8,12},{12,8},{1,5},{5,1},{9,13},{13,9},{2,6},{6,2},{1... | collective-permute-start | bytes 393224 | tf_op jit(solution)/shard_map/ppermute | solution.py:557
  31.3 7.3 %collective-permute-start.9 = (f32[2,4,32,128]{3,2,1,0:T(8,128)S(1)}, f32[2,4,32,128]{3,2,1,0:T(8,128)S(1)}, u32[]{:S(2)}, u32[]{:S(2)}) collective-permute-start(f32[2,4,32,128]{3,2,1,0:T(8,128)S(1)} %get-tuple-element.23), channel_id=1, source_target_pairs={{0,1},{1,0},{2,3},{3,2},{4,5},{5,4},{6,7},{7,6},{8,9},{9,8},{10,11... | collective-permute-start | bytes 393224 | tf_op jit(solution)/shard_map/ppermute | solution.py:569
  31.9 6.7 %collective-permute-start.10 = (f32[2,4,32,128]{3,2,1,0:T(8,128)S(1)}, f32[2,4,32,128]{3,2,1,0:T(8,128)S(1)}, u32[]{:S(2)}, u32[]{:S(2)}) collective-permute-start(f32[2,4,32,128]{3,2,1,0:T(8,128)S(1)} %get-tuple-element.24), channel_id=1, source_target_pairs={{0,2},{1,3},{2,0},{3,1},{4,6},{5,7},{6,4},{7,5},{8,10},{9,11},{10,... | collective-permute-start | bytes 393224 | tf_op jit(solution)/shard_map/ppermute | solution.py:569
  32.4 6.2 %collective-permute-start.11 = (f32[2,4,32,128]{3,2,1,0:T(8,128)S(1)}, f32[2,4,32,128]{3,2,1,0:T(8,128)S(1)}, u32[]{:S(2)}, u32[]{:S(2)}) collective-permute-start(f32[2,4,32,128]{3,2,1,0:T(8,128)S(1)} %get-tuple-element.25), channel_id=1, source_target_pairs={{0,3},{1,2},{2,1},{3,0},{4,7},{5,6},{6,5},{7,4},{8,11},{9,10},{10,... | collective-permute-start | bytes 393224 | tf_op jit(solution)/shard_map/ppermute | solution.py:569
  43.0 6.2 %collective-permute-start.12 = (f32[2,4,32,128]{3,2,1,0:T(8,128)S(1)}, f32[2,4,32,128]{3,2,1,0:T(8,128)S(1)}, u32[]{:S(2)}, u32[]{:S(2)}) collective-permute-start(f32[2,4,32,128]{3,2,1,0:T(8,128)S(1)} %shard_map.98), channel_id=1, source_target_pairs={{0,1},{1,0},{2,3},{3,2},{4,5},{5,4},{6,7},{7,6},{8,9},{9,8},{10,11... | collective-permute-start | bytes 393224 | tf_op jit(solution)/shard_map/ppermute | solution.py:569
  45.3 5.6 %collective-permute-start.13 = (f32[2,4,32,128]{3,2,1,0:T(8,128)S(1)}, f32[2,4,32,128]{3,2,1,0:T(8,128)S(1)}, u32[]{:S(2)}, u32[]{:S(2)}) collective-permute-start(f32[2,4,32,128]{3,2,1,0:T(8,128)S(1)} %shard_map.99), channel_id=1, source_target_pairs={{0,2},{1,3},{2,0},{3,1},{4,6},{5,7},{6,4},{7,5},{8,10},{9,11},{10,... | collective-permute-start | bytes 393224 | tf_op jit(solution)/shard_map/ppermute | solution.py:569
  47.4 5.9 %collective-permute-start.14 = (f32[2,4,32,128]{3,2,1,0:T(8,128)S(1)}, f32[2,4,32,128]{3,2,1,0:T(8,128)S(1)}, u32[]{:S(2)}, u32[]{:S(2)}) collective-permute-start(f32[2,4,32,128]{3,2,1,0:T(8,128)S(1)} %shard_map.100), channel_id=1, source_target_pairs={{0,3},{1,2},{2,1},{3,0},{4,7},{5,6},{6,5},{7,4},{8,11},{9,10},{10,... | collective-permute-start | bytes 393224 | tf_op jit(solution)/shard_map/ppermute | solution.py:569
  48.9 4.4 %collective-permute-start.15 = (f32[2,4,32,128]{3,2,1,0:T(8,128)S(1)}, f32[2,4,32,128]{3,2,1,0:T(8,128)S(1)}, u32[]{:S(2)}, u32[]{:S(2)}) collective-permute-start(f32[2,4,32,128]{3,2,1,0:T(8,128)S(1)} %shard_map.97.refs_0_), channel_id=1, source_target_pairs={{0,16},{16,0},{1,17},{17,1},{2,18},{18,2},{3,19},{19,3},{4,20},{20... | collective-permute-start | bytes 393224 | tf_op jit(solution)/shard_map/ppermute | solution.py:565
  49.2 4.1 %collective-permute-start.16 = (f32[2,4,32,128]{3,2,1,0:T(8,128)S(1)}, f32[2,4,32,128]{3,2,1,0:T(8,128)S(1)}, u32[]{:S(2)}, u32[]{:S(2)}) collective-permute-start(f32[2,4,32,128]{3,2,1,0:T(8,128)S(1)} %collective-permute-done.12.refs_1_), channel_id=1, source_target_pairs={{0,16},{16,0},{1,17},{17,1},{2,18},{18,2},{3,19},{19,3},{4,20},{20... | collective-permute-start | bytes 393224 | tf_op jit(solution)/shard_map/ppermute | solution.py:565
  50.9 2.5 %collective-permute-start.17 = (f32[2,4,32,128]{3,2,1,0:T(8,128)S(1)}, f32[2,4,32,128]{3,2,1,0:T(8,128)S(1)}, u32[]{:S(2)}, u32[]{:S(2)}) collective-permute-start(f32[2,4,32,128]{3,2,1,0:T(8,128)S(1)} %collective-permute-done.13.refs_2_), channel_id=1, source_target_pairs={{0,16},{16,0},{1,17},{17,1},{2,18},{18,2},{3,19},{19,3},{4,20},{20... | collective-permute-start | bytes 393224 | tf_op jit(solution)/shard_map/ppermute | solution.py:565
  53.4 1.3 %collective-permute-start.18 = (f32[2,4,32,128]{3,2,1,0:T(8,128)S(1)}, f32[2,4,32,128]{3,2,1,0:T(8,128)S(1)}, u32[]{:S(2)}, u32[]{:S(2)}) collective-permute-start(f32[2,4,32,128]{3,2,1,0:T(8,128)S(1)} %collective-permute-done.14.refs_3_), channel_id=1, source_target_pairs={{0,16},{16,0},{1,17},{17,1},{2,18},{18,2},{3,19},{19,3},{4,20},{20... | collective-permute-start | bytes 393224 | tf_op jit(solution)/shard_map/ppermute | solution.py:565
where the time goes:
time: 56.3 us; the launch traced here: 56.1 us
  starting transfers between devices  23.7 us (42%)
  Pallas kernels  16.4 us (29%)
  waiting for transfers between devices  14.8 us (26%)
  local copies, waits for them, and re-layouts  0.91 us (2%)
    pallas_call x10, Pallas kernels, call(): pl.pallas_call(kernel, in_specs=[pl.BlockSpec(memory_space=pltpu.SMEM)] +...  15 us
    ppermute x4, starting transfers between devices, trade(): return lax.ppermute(value, 'tile', pairs)  12.1 us
    ppermute x9, starting transfers between devices, over_mem(): lax.ppermute(value, 'mem', [(i, i ^ k) for i in range(lax.axis_size('mem'...  10.7 us
    ppermute x9, waiting for transfers between devices, over_mem(): lax.ppermute(value, 'mem', [(i, i ^ k) for i in range(lax.axis_size('mem'...  8.54 us
    ppermute x4, waiting for transfers between devices, trade(): return lax.ppermute(value, 'tile', pairs)  4.28 us
    ppermute x6, waiting for transfers between devices, to_partner(): return lax.ppermute(value, 'section', [(0, 1), (1, 0)])  2.01 us
    pallas_call x1, Pallas kernels, unpack(): pl.pallas_call(functools.partial(unpack_kernel, share, mems), in_specs=[p...  1.4 us
  transfers between devices with their start and end apart: 19, of which 9 were waited for; matrix products, arithmetic and copies ran while one was open for 2% of the time, Pallas kernels for 10%

commit v1 on v0

--- a/solution.py
+++ b/solution.py
@@ -22,17 +22,27 @@
 CENTRE, PARITY, SECTION, MEM, HAS_A, HAS_B, TILE_X = range(7)
 
 
+def position(tiles, width_x, share, mems):
+    tile, section, mem = (lax.axis_index(name) for name in ("tile", "section", "mem"))
+    parity = tile % 2
+    above, below = (tile < tiles - 1).astype(jnp.int32), (tile > 0).astype(jnp.int32)
+    first = 2 * (tile * width_x + (section * mems + mem) * share) + DB - 1
+    has_a = jnp.where(parity == 1, below, above)
+    has_b = jnp.where(parity == 1, above, below)
+    return first, parity, section, mem, has_a, has_b, tile * width_x
+
+
 def call(kernel, outs, place, *args, scratch=(), inputs=pltpu.VMEM):
     vmem = pl.BlockSpec(memory_space=pltpu.VMEM)
     outs = [pltpu.VMEM(shape, dtype) for shape, dtype in outs]
     return pl.pallas_call(
-        kernel,
-        in_specs=[pl.BlockSpec(memory_space=pltpu.SMEM)] + [vmem] * len(args),
+        lambda *refs: kernel(position(*place), *refs),
+        in_specs=[vmem] * len(args),
         out_specs=[vmem] * len(outs),
         out_shape=outs,
         scratch_shapes=list(scratch),
         compiler_params=pltpu.CompilerParams(vmem_limit_bytes=VMEM_LIMIT),
-    )(place, *[pltpu.with_memory_space_constraint(a, inputs) for a in args])
+    )(*[pltpu.with_memory_space_constraint(a, inputs) for a in args])
 
 
 def split_2(value):
@@ -350,7 +360,8 @@
     )[0]
 
 
-def anomalies(place_ref, keep_ref, other_ref, near_refs, anomaly_ref, base_ref):
+def centre_kernel(place_ref, keep_ref, other_ref, *refs):
+    near_refs, (mean_ref, anomaly_ref, base_ref) = refs[:-3], refs[-3:]
     members, rows, _ = anomaly_ref.shape
     mems = len(near_refs) + 1
     memb_dev = members // (2 * mems)
@@ -369,15 +380,23 @@
             for i in range(memb_dev)
         ]
         mean = sum(field for *_, field in fields) * (1.0 / members)
-        base_ref[at, :] = mean
+        base = mean
         for other, k, i, field in fields:
             member = ((place_ref[SECTION] ^ other) * mems + (place_ref[MEM] ^ k)) * memb_dev + i
-            anomaly_ref[member, at, :] = field - mean
-
-
-def transform_kernel(mems, fields, place_ref, part_ref, za_ref, zb_ref, a_ref, b_ref, weight_ref, *refs):
-    keep_ref, other_ref, near_refs, refs = refs[0], refs[1], refs[2 : mems + 1], refs[mems + 1 :]
-    inv_ref, anomaly_ref, base_ref, y_ref, zh_ref, zl_ref, gram_ref, low_ref, s_ref = refs
+            field = field - mean
+            anomaly_ref[member, at, :] = field
+            base = base + field * mean_ref[pl.ds(member, SUB, stride=0), :]
+        base_ref[at, :] = base
+
+
+def centre(place, keep, other, near, mean):
+    mems, memb_dev, rows, width_y = keep.shape
+    outs = [((2 * mems * memb_dev, rows, width_y), F32), ((rows, width_y), F32)]
+    return call(centre_kernel, outs, place, keep, other, *near, mean)
+
+
+def transform_kernel(fields, place_ref, part_ref, za_ref, zb_ref, a_ref, b_ref, weight_ref, *refs):
+    inv_ref, mean_ref, y_ref, zh_ref, zl_ref, gram_ref, low_ref, s_ref = refs
     obs = y_ref.shape[1]
     members = y_ref.shape[0]
     starts, offsets, total = pair_rows(members)
@@ -386,7 +405,6 @@
         read = info_reader(place_ref, info_ref, fields, n == 0)
         weight = weight_ref[:, pl.ds((n + 1) * obs, obs)]
         sums = sums + gram_of(place_ref, near_ref, read, weight, y_ref, zh_ref, zl_ref)
-    anomalies(place_ref, keep_ref, other_ref, near_refs, anomaly_ref, base_ref)
 
     width = sums.shape[1]
     domain = lax.broadcasted_iota(jnp.int32, (width, LANES), 0) % (width // 2)
@@ -433,26 +451,16 @@
             inv[b] = inv[b] * scale
             inv_ref[k, pl.ds(b * SUB, SUB), :] = inv[b]
             mean[b] = mean[b] + inv[b] * forced
-    for row in range(base_ref.shape[0] // SUB):
-        at = pl.ds(row * SUB, SUB)
-        base = base_ref[at, :]
-        for j in range(members):
-            shift = jnp.broadcast_to(mean[j // SUB][j % SUB : j % SUB + 1, :], (SUB, LANES))
-            base = base + anomaly_ref[j, at, :] * shift
-        base_ref[at, :] = base
-
-
-def transforms(place, part, near_a, near_b, a, b, weight, keep, other, near, fields):
+    for b in range(blocks):
+        mean_ref[pl.ds(b * SUB, SUB), :] = mean[b]
+
+
+def transforms(place, part, near_a, near_b, a, b, weight, fields):
     members, obs = ensemble(near_a)
     _, _, total = pair_rows(members)
-    rows = keep.shape[2]
     return call(
-        functools.partial(transform_kernel, keep.shape[0], fields),
-        [
-            ((members, members, LANES), F32),
-            ((members, rows, LANES), F32),
-            ((rows, LANES), F32),
-        ],
+        functools.partial(transform_kernel, fields),
+        [((members, members, LANES), F32), ((members, LANES), F32)],
         place,
         part,
         near_a,
@@ -460,9 +468,6 @@
         a,
         b,
         weight,
-        keep,
-        other,
-        *near,
         scratch=gram_scratch(members, obs)
         + [
             pltpu.VMEM((total + members, LANES), F32),
@@ -537,14 +542,14 @@
     vmem = pl.BlockSpec(memory_space=pltpu.VMEM)
     shape = (memb_dev, 2 * mems * rows, width_y)
     return pl.pallas_call(
-        functools.partial(unpack_kernel, share, mems),
-        in_specs=[pl.BlockSpec(memory_space=pltpu.SMEM)] + [vmem] * (2 * mems),
+        lambda *refs: unpack_kernel(share, mems, position(*place), *refs),
+        in_specs=[vmem] * (2 * mems),
         out_specs=pl.BlockSpec(memory_space=pltpu.HBM),
         out_shape=jax.ShapeDtypeStruct(shape, F32),
         scratch_shapes=[pltpu.VMEM(shape, F32), pltpu.SemaphoreType.DMA((memb_dev,))],
         compiler_params=pltpu.CompilerParams(vmem_limit_bytes=VMEM_LIMIT),
         name="unpack",
-    )(place, *[pltpu.with_memory_space_constraint(x, pltpu.VMEM) for x in (*near, *far)])
+    )(*[pltpu.with_memory_space_constraint(x, pltpu.VMEM) for x in (*near, *far)])
 
 
 def along_tile(first, second):
@@ -580,23 +585,11 @@
     groups = lax.axis_size(GROUP)
     assert groups == 2 * mems and mems & (mems - 1) == 0
     tiles = lax.axis_size("tile")
-    tile = lax.axis_index("tile")
     group_idx = lax.axis_index(GROUP)
     share = width_x // groups
     far = list(range(mems - 1, 0, -1))
 
-    parity = tile % 2
-    place = jnp.stack(
-        [
-            2 * (tile * width_x + group_idx * share) + DB - 1,
-            parity,
-            lax.axis_index("section"),
-            lax.axis_index("mem"),
-            ((parity == 1) | (tile < tiles - 1)).astype(jnp.int32),
-            jnp.where(parity == 1, tile < tiles - 1, tile > 0).astype(jnp.int32),
-            tile * width_x,
-        ]
-    ).astype(jnp.int32)
+    place = (tiles, width_x, share, mems)
 
     share_d = share // DB
     lists = lax.dynamic_slice_in_dim(obs_list, group_idx * share_d, share_d, 0)
@@ -615,13 +608,14 @@
     gathered = [both_obs] + [over_mem(both_obs, k) for k in far[::-1]]
     gathered = jnp.stack(gathered)
     joined = join(place, keep, other)
-    near = [over_mem(joined[k - 1], k) for k in far[::-1]]
+    near = []
+    for k in far[::-1]:
+        near.append(over_mem(joined[k - 1], k))
     near_a, near_b = along_tile(gathered, gathered)
     weight = weights(place, lists, counts, info, a, b, memb_dev * levels)
     part = own_gram(place, gathered, info, weight)
-    inverse, anomaly, base = transforms(
-        place, part, near_a, near_b, a, b, weight, keep, other, near, memb_dev * levels
-    )
+    inverse, mean = transforms(place, part, near_a, near_b, a, b, weight, memb_dev * levels)
+    anomaly, base = centre(place, keep, other, near, mean)
 
     direct = None
     done, away = [None] * mems, [None] * mems

time: 56.3 us -> 47.1 us (0.84)
  Pallas kernels: 16.4 us -> 11 us
  starting transfers between devices: 23.7 us -> 20.4 us
  waiting for transfers between devices: 14.8 us -> 14 us
    pallas_call x11 -> x12, Pallas kernels: 16.4 us -> 11 us  [the longest x11 10.2 us: call(): pl.pallas_call(lambda *refs: kernel(position(*place), *refs), in_specs=[v...]
    ppermute x4, starting transfers between devices: 12.1 us -> 9.1 us  [trade(): return lax.ppermute(value, 'tile', pairs)]
    ppermute x9, waiting for transfers between devices: 8.54 us -> 7.73 us  [over_mem(): lax.ppermute(value, 'mem', [(i, i ^ k) for i in range(lax.axis_size('mem'...]
  transfers between devices with their start and end apart: 19 -> 19, of which waited for: 9 -> 10; matrix products, arithmetic and copies ran while one was open for 2% -> 2% of each run, Pallas kernels for 10% -> 12%
where the time goes in v1:
time: 47.1 us; the launch traced here: 46.6 us
  starting transfers between devices  20.4 us (43%)
  waiting for transfers between devices  14 us (30%)
  Pallas kernels  11 us (23%)
  local copies, waits for them, and re-layouts  0.83 us (2%)
    ppermute x9, starting transfers between devices, over_mem(): lax.ppermute(value, 'mem', [(i, i ^ k) for i in range(lax.axis_size('mem'...  10.7 us
    pallas_call x11, Pallas kernels, call(): pl.pallas_call(lambda *refs: kernel(position(*place), *refs), in_specs=[v...  10.2 us
    ppermute x4, starting transfers between devices, trade(): return lax.ppermute(value, 'tile', pairs)  9.1 us
    ppermute x9, waiting for transfers between devices, over_mem(): lax.ppermute(value, 'mem', [(i, i ^ k) for i in range(lax.axis_size('mem'...  7.73 us
    ppermute x4, waiting for transfers between devices, trade(): return lax.ppermute(value, 'tile', pairs)  4.28 us
    ppermute x6, waiting for transfers between devices, to_partner(): return lax.ppermute(value, 'section', [(0, 1), (1, 0)])  2.02 us
  transfers between devices with their start and end apart: 19, of which 10 were waited for; matrix products, arithmetic and copies ran while one was open for 2% of the time, Pallas kernels for 12%

profile of v1, /device:TPU:0, one launch (start us, length us, event | category | flops | bytes accessed | tf_op | source)
XLA Modules:
  0.0 46.6 jit_solution(15808913477026523485)
XLA Ops:
  0.0 0.0 copy-start
  0.0 0.0 copy-start.1
  0.0 0.0 copy-start.2
  0.0 0.0 copy-start.3
  0.0 0.0 copy-start.4
  0.0 1.4 %shard_map.91 = (f32[97,4,128]{2,1,0:T(4,128)S(1)}, f32[97,4,128]{2,1,0:T(4,128)S(1)}, f32[32,128]{1,0:T(8,128)S(1)}) custom-call(f32[64,16,128]{2,1,0:T(8,128)} %bitcast.17, f32[16,16,128]{2,1,0:T(8,128)} %refs_3_.3, f32[16,16,128]{2,1,0:T(8,128)} %refs_4_.1, f32[16,128]{1,0:T(8,128)} %refs_5_.1, s32[8,128]{1,0:T(8,128)} %bitcast.19, f32[8,128]{1,0:T(8,128)} %bitcast.26, ...), custom_call_target="tpu_custom_call" | custom-call | tf_op jit(solution)/shard_map/pallas_call | solution.py:38
  1.4 0.0 copy-start.5
  1.4 3.1 %collective-permute-start = (f32[97,4,128]{2,1,0:T(4,128)S(1)}, f32[97,4,128]{2,1,0:T(4,128)S(1)}, u32[]{:S(2)}, u32[]{:S(2)}) collective-permute-start(f32[97,4,128]{2,1,0:T(4,128)S(1)} %get-tuple-element.18), channel_id=1, source_target_pairs={{0,4},{4,0},{8,12},{12,8},{1,5},{5,1},{9,13},{13,9},{2,6},{6,2},{1... | collective-permute-start | bytes 595976 | tf_op jit(solution)/shard_map/ppermute | solution.py:562
  4.5 0.7 %collective-permute-start.1 = (f32[97,4,128]{2,1,0:T(4,128)S(1)}, f32[97,4,128]{2,1,0:T(4,128)S(1)}, u32[]{:S(2)}, u32[]{:S(2)}) collective-permute-start(f32[97,4,128]{2,1,0:T(4,128)S(1)} %get-tuple-element.19), channel_id=1, source_target_pairs={{4,8},{8,4},{5,9},{9,5},{6,10},{10,6},{7,11},{11,7},{20,24},{24,20... | collective-permute-start | bytes 595976 | tf_op jit(solution)/shard_map/ppermute | solution.py:562
  5.2 4.3 %collective-permute-done.refs_1_.refs_3_ = f32[97,4,128]{2,1,0:T(4,128)S(1)} collective-permute-done((f32[97,4,128]{2,1,0:T(4,128)S(1)}, f32[97,4,128]{2,1,0:T(4,128)S(1)}, u32[]{:S(2)}, u32[]{:S(2)}) %collective-permute-start) | collective-permute-done | bytes 198688 | tf_op jit(solution)/shard_map/ppermute | solution.py:562
  9.5 0.0 collective-permute-done.1.refs_2_.refs_4_
  9.5 0.0 copy-done.1
  9.5 0.0 copy-done.2
  9.5 0.0 copy-done.3
  9.5 0.0 copy-done.4
  9.5 0.0 copy-done.5
  9.5 2.9 %shard_map.92 = (f32[4,4,32,128]{3,2,1,0:T(8,128)S(1)}, f32[4,4,32,128]{3,2,1,0:T(8,128)S(1)}, f32[4,1024]{1,0:T(4,128)S(1)}) custom-call(f32[64,16,128]{2,1,0:T(8,128)S(1)} %bitcast.18, f32[97,4,128]{2,1,0:T(4,128)S(1)} %collective-permute-done.refs_1_.refs_3_, f32[97,4,128]{2,1,0:T(4,128)S(1)} %collective-permute-done.1.refs_2_.refs_4_, ...), custom_call_target="tpu_custom_call" | custom-call | tf_op jit(solution)/shard_map/pallas_call | solution.py:38
  12.5 0.1 collective-permute-start.6
  12.5 0.5 %collective-permute-start.2 = (f32[4,4,32,128]{3,2,1,0:T(8,128)S(1)}, f32[4,4,32,128]{3,2,1,0:T(8,128)S(1)}, u32[]{:S(2)}, u32[]{:S(2)}) collective-permute-start(f32[4,4,32,128]{3,2,1,0:T(8,128)S(1)} %get-tuple-element.21), channel_id=1, source_target_pairs={{0,16},{16,0},{1,17},{17,1},{2,18},{18,2},{3,19},{19,3},{4,20},{20... | collective-permute-start | bytes 786440 | tf_op jit(solution)/shard_map/ppermute | solution.py:570
  13.0 0.7 %collective-permute-done.6 = f32[4,1024]{1,0:T(4,128)S(1)} collective-permute-done((f32[4,1024]{1,0:T(4,128)S(1)}, f32[4,1024]{1,0:T(4,128)S(1)}, u32[]{:S(2)}, u32[]{:S(2)}) %collective-permute-start.6) | collective-permute-done | bytes 16416 | tf_op jit(solution)/shard_map/ppermute | solution.py:570
  13.7 2.7 %collective-permute-start.9 = (f32[2,4,1024]{2,1,0:T(4,128)S(1)}, f32[2,4,1024]{2,1,0:T(4,128)S(1)}, u32[]{:S(2)}, u32[]{:S(2)}) collective-permute-start(f32[2,4,1024]{2,1,0:T(4,128)S(1)} %get-tuple-element.32), channel_id=1, source_target_pairs={{0,3},{1,2},{2,1},{3,0},{4,7},{5,6},{6,5},{7,4},{8,11},{9,10},{10,... | collective-permute-start | bytes 98312 | tf_op jit(solution)/shard_map/ppermute | solution.py:574
  16.4 0.5 %collective-permute-start.7 = (f32[2,4,1024]{2,1,0:T(4,128)S(1)}, f32[2,4,1024]{2,1,0:T(4,128)S(1)}, u32[]{:S(2)}, u32[]{:S(2)}) collective-permute-start(f32[2,4,1024]{2,1,0:T(4,128)S(1)} %get-tuple-element.32), channel_id=1, source_target_pairs={{0,1},{1,0},{2,3},{3,2},{4,5},{5,4},{6,7},{7,6},{8,9},{9,8},{10,11... | collective-permute-start | bytes 98312 | tf_op jit(solution)/shard_map/ppermute | solution.py:574
  16.9 0.3 collective-permute-start.8
  17.3 1.3 %collective-permute-done.9 = f32[2,4,1024]{2,1,0:T(4,128)S(1)} collective-permute-done((f32[2,4,1024]{2,1,0:T(4,128)S(1)}, f32[2,4,1024]{2,1,0:T(4,128)S(1)}, u32[]{:S(2)}, u32[]{:S(2)}) %collective-permute-start.9) | collective-permute-done | bytes 32800 | tf_op jit(solution)/shard_map/ppermute | solution.py:574
  18.6 1.7 %collective-permute-done.7 = f32[2,4,1024]{2,1,0:T(4,128)S(1)} collective-permute-done((f32[2,4,1024]{2,1,0:T(4,128)S(1)}, f32[2,4,1024]{2,1,0:T(4,128)S(1)}, u32[]{:S(2)}, u32[]{:S(2)}) %collective-permute-start.7) | collective-permute-done | bytes 32800 | tf_op jit(solution)/shard_map/ppermute | solution.py:574
  20.3 0.5 %collective-permute-done.8 = f32[2,4,1024]{2,1,0:T(4,128)S(1)} collective-permute-done((f32[2,4,1024]{2,1,0:T(4,128)S(1)}, f32[2,4,1024]{2,1,0:T(4,128)S(1)}, u32[]{:S(2)}, u32[]{:S(2)}) %collective-permute-start.8) | collective-permute-done | bytes 32800 | tf_op jit(solution)/shard_map/ppermute | solution.py:574
  20.9 4.7 %collective-permute-start.10 = (f32[4,2,4,1024]{3,2,1,0:T(4,128)S(1)}, f32[4,2,4,1024]{3,2,1,0:T(4,128)S(1)}, u32[]{:S(2)}, u32[]{:S(2)}) collective-permute-start(f32[4,2,4,1024]{3,2,1,0:T(4,128)S(1)} %pad_maximum_fusion.refs_0_), channel_id=1, source_target_pairs={{0,4},{4,0},{8,12},{12,8},{1,5},{5,1},{9,13},{13,9},{2,6},{6,2},{1... | collective-permute-start | bytes 393224 | tf_op jit(solution)/shard_map/ppermute | solution.py:562
  25.5 0.7 %collective-permute-start.11 = (f32[4,2,4,1024]{3,2,1,0:T(4,128)S(1)}, f32[4,2,4,1024]{3,2,1,0:T(4,128)S(1)}, u32[]{:S(2)}, u32[]{:S(2)}) collective-permute-start(f32[4,2,4,1024]{3,2,1,0:T(4,128)S(1)} %pad_maximum_fusion.refs_0_), channel_id=1, source_target_pairs={{4,8},{8,4},{5,9},{9,5},{6,10},{10,6},{7,11},{11,7},{20,24},{24,20... | collective-permute-start | bytes 393224 | tf_op jit(solution)/shard_map/ppermute | solution.py:562
  26.2 0.0 collective-permute-done.2.refs_1_
  26.2 1.6 %collective-permute-start.3 = (f32[2,4,32,128]{3,2,1,0:T(8,128)S(1)}, f32[2,4,32,128]{3,2,1,0:T(8,128)S(1)}, u32[]{:S(2)}, u32[]{:S(2)}) collective-permute-start(f32[2,4,32,128]{3,2,1,0:T(8,128)S(1)} %get-tuple-element.22), channel_id=1, source_target_pairs={{0,1},{1,0},{2,3},{3,2},{4,5},{5,4},{6,7},{7,6},{8,9},{9,8},{10,11... | collective-permute-start | bytes 393224 | tf_op jit(solution)/shard_map/ppermute | solution.py:574
  27.8 0.5 %collective-permute-start.4 = (f32[2,4,32,128]{3,2,1,0:T(8,128)S(1)}, f32[2,4,32,128]{3,2,1,0:T(8,128)S(1)}, u32[]{:S(2)}, u32[]{:S(2)}) collective-permute-start(f32[2,4,32,128]{3,2,1,0:T(8,128)S(1)} %get-tuple-element.23), channel_id=1, source_target_pairs={{0,2},{1,3},{2,0},{3,1},{4,6},{5,7},{6,4},{7,5},{8,10},{9,11},{10,... | collective-permute-start | bytes 393224 | tf_op jit(solution)/shard_map/ppermute | solution.py:574
  28.3 1.5 %collective-permute-start.5 = (f32[2,4,32,128]{3,2,1,0:T(8,128)S(1)}, f32[2,4,32,128]{3,2,1,0:T(8,128)S(1)}, u32[]{:S(2)}, u32[]{:S(2)}) collective-permute-start(f32[2,4,32,128]{3,2,1,0:T(8,128)S(1)} %get-tuple-element.24), channel_id=1, source_target_pairs={{0,3},{1,2},{2,1},{3,0},{4,7},{5,6},{6,5},{7,4},{8,11},{9,10},{10,... | collective-permute-start | bytes 393224 | tf_op jit(solution)/shard_map/ppermute | solution.py:574
  29.8 0.7 %dynamic-slice_bitcast_fusion.1 = s32[64,1]{0,1:T(1,128)S(1)} fusion(s32[8,64]{1,0:T(8,128)} %param.17, s32[]{:T(128)S(6)} %select_n.4), kind=kLoop, calls=%fused_computation.3 | loop fusion | bytes 516 | tf_op jit(solution)/shard_map/reshape | solution.py:597
  30.5 0.1 copy.10.refs_1_
  30.6 0.0 copy-done
  30.6 0.9 %shard_map.94.refs_2_.refs_5_ = bf16[128,3072]{1,0:T(8,128)(2,1)S(1)} custom-call(s32[64,256]{1,0:T(8,128)S(1)} %dynamic-slice_bitcast_fusion.refs_0_, s32[64,1]{1,0:T(8,128)S(1)} %copy.10.refs_1_, f32[32,128]{1,0:T(8,128)S(1)} %get-tuple-element.26.refs_2_.refs_1_, f32[97,4,128]{2,1,0:T(4,128)S(1)} %collective-permute-done.refs_1_.refs_3_, ...), custom_call_target="tpu_custom_call" | custom-call | tf_op jit(solution)/shard_map/pallas_call | solution.py:38
  31.5 0.9 %shard_map.95.refs_0_ = f32[672,128]{1,0:T(8,128)S(1)} custom-call(f32[4,2,4,1024]{3,2,1,0:T(4,128)S(1)} %pad_maximum_fusion.refs_0_, f32[32,128]{1,0:T(8,128)S(1)} %get-tuple-element.26.refs_2_.refs_1_, bf16[128,3072]{1,0:T(8,128)(2,1)S(1)} %shard_map.94.refs_2_.refs_5_), custom_call_target="tpu_custom_call" | custom-call | tf_op jit(solution)/shard_map/pallas_call | solution.py:38
  32.4 0.0 collective-permute-done.10.refs_1_
  32.4 0.0 collective-permute-done.11.refs_2_
  32.4 3.0 %shard_map.96 = (f32[32,32,128]{2,1,0:T(8,128)S(1)}, f32[32,128]{1,0:T(8,128)S(1)}) custom-call(f32[672,128]{1,0:T(8,128)S(1)} %shard_map.95.refs_0_, f32[4,2,4,1024]{3,2,1,0:T(4,128)S(1)} %collective-permute-done.10.refs_1_, f32[4,2,4,1024]{3,2,1,0:T(4,128)S(1)} %collective-permute-done.11.refs_2_, f32[97,4,128]{2,1,0:T(4,128)S(1)} %collective-permute-done.refs_1_.refs_3_, ...), custom_call_target="tpu_custom_call" | custom-call | tf_op jit(solution)/shard_map/pallas_call | solution.py:38
  35.5 0.0 collective-permute-done.3.refs_2_
  35.5 0.0 collective-permute-done.4.refs_3_
  35.5 0.0 collective-permute-done.5.refs_4_
  35.5 0.2 shard_map.97
  35.7 0.3 shard_map.101
  36.0 1.4 %collective-permute-start.14 = (f32[2,4,32,128]{3,2,1,0:T(8,128)S(1)}, f32[2,4,32,128]{3,2,1,0:T(8,128)S(1)}, u32[]{:S(2)}, u32[]{:S(2)}) collective-permute-start(f32[2,4,32,128]{3,2,1,0:T(8,128)S(1)} %shard_map.101), channel_id=1, source_target_pairs={{0,3},{1,2},{2,1},{3,0},{4,7},{5,6},{6,5},{7,4},{8,11},{9,10},{10,... | collective-permute-start | bytes 393224 | tf_op jit(solution)/shard_map/ppermute | solution.py:574
  37.4 0.2 shard_map.100
  37.6 1.6 %collective-permute-start.13 = (f32[2,4,32,128]{3,2,1,0:T(8,128)S(1)}, f32[2,4,32,128]{3,2,1,0:T(8,128)S(1)}, u32[]{:S(2)}, u32[]{:S(2)}) collective-permute-start(f32[2,4,32,128]{3,2,1,0:T(8,128)S(1)} %shard_map.100), channel_id=1, source_target_pairs={{0,2},{1,3},{2,0},{3,1},{4,6},{5,7},{6,4},{7,5},{8,10},{9,11},{10,... | collective-permute-start | bytes 393224 | tf_op jit(solution)/shard_map/ppermute | solution.py:574
  39.2 0.2 shard_map.99
  39.4 0.6 %collective-permute-start.12 = (f32[2,4,32,128]{3,2,1,0:T(8,128)S(1)}, f32[2,4,32,128]{3,2,1,0:T(8,128)S(1)}, u32[]{:S(2)}, u32[]{:S(2)}) collective-permute-start(f32[2,4,32,128]{3,2,1,0:T(8,128)S(1)} %shard_map.99), channel_id=1, source_target_pairs={{0,1},{1,0},{2,3},{3,2},{4,5},{5,4},{6,7},{7,6},{8,9},{9,8},{10,11... | collective-permute-start | bytes 393224 | tf_op jit(solution)/shard_map/ppermute | solution.py:574
  40.0 0.1 shard_map.98.refs_0_
  40.2 0.1 collective-permute-start.15
  40.3 1.8 %collective-permute-done.14.refs_3_ = f32[2,4,32,128]{3,2,1,0:T(8,128)S(1)} collective-permute-done((f32[2,4,32,128]{3,2,1,0:T(8,128)S(1)}, f32[2,4,32,128]{3,2,1,0:T(8,128)S(1)}, u32[]{:S(2)}, u32[]{:S(2)}) %collective-permute-start.14) | collective-permute-done | bytes 131104 | tf_op jit(solution)/shard_map/ppermute | solution.py:574
  42.0 0.0 collective-permute-start.18
  42.0 1.3 %collective-permute-done.13.refs_2_ = f32[2,4,32,128]{3,2,1,0:T(8,128)S(1)} collective-permute-done((f32[2,4,32,128]{3,2,1,0:T(8,128)S(1)}, f32[2,4,32,128]{3,2,1,0:T(8,128)S(1)}, u32[]{:S(2)}, u32[]{:S(2)}) %collective-permute-start.13) | collective-permute-done | bytes 131104 | tf_op jit(solution)/shard_map/ppermute | solution.py:574
  43.4 0.0 collective-permute-start.17
  43.4 1.0 %collective-permute-done.12.refs_1_ = f32[2,4,32,128]{3,2,1,0:T(8,128)S(1)} collective-permute-done((f32[2,4,32,128]{3,2,1,0:T(8,128)S(1)}, f32[2,4,32,128]{3,2,1,0:T(8,128)S(1)}, u32[]{:S(2)}, u32[]{:S(2)}) %collective-permute-start.12) | collective-permute-done | bytes 131104 | tf_op jit(solution)/shard_map/ppermute | solution.py:574
  44.4 0.0 collective-permute-start.16
  44.4 0.0 collective-permute-done.15.refs_4_
  44.4 0.0 collective-permute-done.18.refs_7_
  44.4 0.3 collective-permute-done.17.refs_6_
  44.7 1.0 %collective-permute-done.16.refs_5_ = f32[2,4,32,128]{3,2,1,0:T(8,128)S(1)} collective-permute-done((f32[2,4,32,128]{3,2,1,0:T(8,128)S(1)}, f32[2,4,32,128]{3,2,1,0:T(8,128)S(1)}, u32[]{:S(2)}, u32[]{:S(2)}) %collective-permute-start.16) | collective-permute-done | bytes 131104 | tf_op jit(solution)/shard_map/ppermute | solution.py:570
  45.8 0.9 %unpack.1 = f32[4,256,128]{2,1,0:T(8,128)} custom-call(f32[2,4,32,128]{3,2,1,0:T(8,128)S(1)} %shard_map.98.refs_0_, f32[2,4,32,128]{3,2,1,0:T(8,128)S(1)} %collective-permute-done.12.refs_1_, f32[2,4,32,128]{3,2,1,0:T(8,128)S(1)} %collective-permute-done.13.refs_2_, f32[2,4,32,128]{3,2,1,0:T(8,128)S(1)} %collective-permute-done.14.refs_3_, ...), custom_call_target="tpu_custom_call" | custom-call | tf_op jit(solution)/shard_map/unpack/pallas_call | solution.py:544
  (4 shorter events, 0.1 us)
Async XLA Ops:
  0.0 30.6 %copy-start = (s32[8,64,256]{2,1,0:T(8,128)S(1)}, s32[8,64,256]{2,1,0:T(8,128)}, u32[]{:S(2)}) copy-start(s32[8,64,256]{2,1,0:T(8,128)} %param.16) | copy-start | bytes 1572868
  0.0 9.5 %copy-start.1 = (f32[4,16,16,128]{3,2,1,0:T(8,128)S(1)}, f32[4,16,16,128]{3,2,1,0:T(8,128)}, u32[]{:S(2)}) copy-start(f32[4,16,16,128]{3,2,1,0:T(8,128)} %param.9) | copy-start | bytes 1572868
  0.0 9.5 %copy-start.2 = (f32[16,16,128]{2,1,0:T(8,128)S(1)}, f32[16,16,128]{2,1,0:T(8,128)}, u32[]{:S(2)}) copy-start(f32[16,16,128]{2,1,0:T(8,128)} %refs_3_.3) | copy-start | bytes 393220
  0.0 9.5 %copy-start.3 = (f32[16,16,128]{2,1,0:T(8,128)S(1)}, f32[16,16,128]{2,1,0:T(8,128)}, u32[]{:S(2)}) copy-start(f32[16,16,128]{2,1,0:T(8,128)} %refs_4_.1) | copy-start | bytes 393220
  0.0 9.5 %copy-start.4 = (f32[16,128]{1,0:T(8,128)S(1)}, f32[16,128]{1,0:T(8,128)}, u32[]{:S(2)}) copy-start(f32[16,128]{1,0:T(8,128)} %refs_5_.1) | copy-start | bytes 24580
  1.4 8.1 %copy-start.5 = (s32[1024]{0:T(1024)S(1)}, s32[1024]{0:T(1024)}, u32[]{:S(2)}) copy-start(s32[1024]{0:T(1024)} %param.13) | copy-start | bytes 12292
  1.4 8.1 %collective-permute-start = (f32[97,4,128]{2,1,0:T(4,128)S(1)}, f32[97,4,128]{2,1,0:T(4,128)S(1)}, u32[]{:S(2)}, u32[]{:S(2)}) collective-permute-start(f32[97,4,128]{2,1,0:T(4,128)S(1)} %get-tuple-element.18), channel_id=1, source_target_pairs={{0,4},{4,0},{8,12},{12,8},{1,5},{5,1},{9,13},{13,9},{2,6},{6,2},{1... | collective-permute-start | bytes 595976 | tf_op jit(solution)/shard_map/ppermute | solution.py:562
  4.5 4.9 %collective-permute-start.1 = (f32[97,4,128]{2,1,0:T(4,128)S(1)}, f32[97,4,128]{2,1,0:T(4,128)S(1)}, u32[]{:S(2)}, u32[]{:S(2)}) collective-permute-start(f32[97,4,128]{2,1,0:T(4,128)S(1)} %get-tuple-element.19), channel_id=1, source_target_pairs={{4,8},{8,4},{5,9},{9,5},{6,10},{10,6},{7,11},{11,7},{20,24},{24,20... | collective-permute-start | bytes 595976 | tf_op jit(solution)/shard_map/ppermute | solution.py:562
  12.5 1.2 %collective-permute-start.6 = (f32[4,1024]{1,0:T(4,128)S(1)}, f32[4,1024]{1,0:T(4,128)S(1)}, u32[]{:S(2)}, u32[]{:S(2)}) collective-permute-start(f32[4,1024]{1,0:T(4,128)S(1)} %get-tuple-element.25), channel_id=1, source_target_pairs={{0,16},{16,0},{1,17},{17,1},{2,18},{18,2},{3,19},{19,3},{4,20},{20... | collective-permute-start | bytes 49160 | tf_op jit(solution)/shard_map/ppermute | solution.py:570
  12.5 13.7 %collective-permute-start.2 = (f32[4,4,32,128]{3,2,1,0:T(8,128)S(1)}, f32[4,4,32,128]{3,2,1,0:T(8,128)S(1)}, u32[]{:S(2)}, u32[]{:S(2)}) collective-permute-start(f32[4,4,32,128]{3,2,1,0:T(8,128)S(1)} %get-tuple-element.21), channel_id=1, source_target_pairs={{0,16},{16,0},{1,17},{17,1},{2,18},{18,2},{3,19},{19,3},{4,20},{20... | collective-permute-start | bytes 786440 | tf_op jit(solution)/shard_map/ppermute | solution.py:570
  13.7 4.9 %collective-permute-start.9 = (f32[2,4,1024]{2,1,0:T(4,128)S(1)}, f32[2,4,1024]{2,1,0:T(4,128)S(1)}, u32[]{:S(2)}, u32[]{:S(2)}) collective-permute-start(f32[2,4,1024]{2,1,0:T(4,128)S(1)} %get-tuple-element.32), channel_id=1, source_target_pairs={{0,3},{1,2},{2,1},{3,0},{4,7},{5,6},{6,5},{7,4},{8,11},{9,10},{10,... | collective-permute-start | bytes 98312 | tf_op jit(solution)/shard_map/ppermute | solution.py:574
  16.4 3.9 %collective-permute-start.7 = (f32[2,4,1024]{2,1,0:T(4,128)S(1)}, f32[2,4,1024]{2,1,0:T(4,128)S(1)}, u32[]{:S(2)}, u32[]{:S(2)}) collective-permute-start(f32[2,4,1024]{2,1,0:T(4,128)S(1)} %get-tuple-element.32), channel_id=1, source_target_pairs={{0,1},{1,0},{2,3},{3,2},{4,5},{5,4},{6,7},{7,6},{8,9},{9,8},{10,11... | collective-permute-start | bytes 98312 | tf_op jit(solution)/shard_map/ppermute | solution.py:574
  16.9 3.9 %collective-permute-start.8 = (f32[2,4,1024]{2,1,0:T(4,128)S(1)}, f32[2,4,1024]{2,1,0:T(4,128)S(1)}, u32[]{:S(2)}, u32[]{:S(2)}) collective-permute-start(f32[2,4,1024]{2,1,0:T(4,128)S(1)} %get-tuple-element.32), channel_id=1, source_target_pairs={{0,2},{1,3},{2,0},{3,1},{4,6},{5,7},{6,4},{7,5},{8,10},{9,11},{10,... | collective-permute-start | bytes 98312 | tf_op jit(solution)/shard_map/ppermute | solution.py:574
  20.9 11.5 %collective-permute-start.10 = (f32[4,2,4,1024]{3,2,1,0:T(4,128)S(1)}, f32[4,2,4,1024]{3,2,1,0:T(4,128)S(1)}, u32[]{:S(2)}, u32[]{:S(2)}) collective-permute-start(f32[4,2,4,1024]{3,2,1,0:T(4,128)S(1)} %pad_maximum_fusion.refs_0_), channel_id=1, source_target_pairs={{0,4},{4,0},{8,12},{12,8},{1,5},{5,1},{9,13},{13,9},{2,6},{6,2},{1... | collective-permute-start | bytes 393224 | tf_op jit(solution)/shard_map/ppermute | solution.py:562
  25.5 6.9 %collective-permute-start.11 = (f32[4,2,4,1024]{3,2,1,0:T(4,128)S(1)}, f32[4,2,4,1024]{3,2,1,0:T(4,128)S(1)}, u32[]{:S(2)}, u32[]{:S(2)}) collective-permute-start(f32[4,2,4,1024]{3,2,1,0:T(4,128)S(1)} %pad_maximum_fusion.refs_0_), channel_id=1, source_target_pairs={{4,8},{8,4},{5,9},{9,5},{6,10},{10,6},{7,11},{11,7},{20,24},{24,20... | collective-permute-start | bytes 393224 | tf_op jit(solution)/shard_map/ppermute | solution.py:562
  26.2 9.2 %collective-permute-start.3 = (f32[2,4,32,128]{3,2,1,0:T(8,128)S(1)}, f32[2,4,32,128]{3,2,1,0:T(8,128)S(1)}, u32[]{:S(2)}, u32[]{:S(2)}) collective-permute-start(f32[2,4,32,128]{3,2,1,0:T(8,128)S(1)} %get-tuple-element.22), channel_id=1, source_target_pairs={{0,1},{1,0},{2,3},{3,2},{4,5},{5,4},{6,7},{7,6},{8,9},{9,8},{10,11... | collective-permute-start | bytes 393224 | tf_op jit(solution)/shard_map/ppermute | solution.py:574
  27.8 7.7 %collective-permute-start.4 = (f32[2,4,32,128]{3,2,1,0:T(8,128)S(1)}, f32[2,4,32,128]{3,2,1,0:T(8,128)S(1)}, u32[]{:S(2)}, u32[]{:S(2)}) collective-permute-start(f32[2,4,32,128]{3,2,1,0:T(8,128)S(1)} %get-tuple-element.23), channel_id=1, source_target_pairs={{0,2},{1,3},{2,0},{3,1},{4,6},{5,7},{6,4},{7,5},{8,10},{9,11},{10,... | collective-permute-start | bytes 393224 | tf_op jit(solution)/shard_map/ppermute | solution.py:574
  28.3 7.2 %collective-permute-start.5 = (f32[2,4,32,128]{3,2,1,0:T(8,128)S(1)}, f32[2,4,32,128]{3,2,1,0:T(8,128)S(1)}, u32[]{:S(2)}, u32[]{:S(2)}) collective-permute-start(f32[2,4,32,128]{3,2,1,0:T(8,128)S(1)} %get-tuple-element.24), channel_id=1, source_target_pairs={{0,3},{1,2},{2,1},{3,0},{4,7},{5,6},{6,5},{7,4},{8,11},{9,10},{10,... | collective-permute-start | bytes 393224 | tf_op jit(solution)/shard_map/ppermute | solution.py:574
  36.0 6.1 %collective-permute-start.14 = (f32[2,4,32,128]{3,2,1,0:T(8,128)S(1)}, f32[2,4,32,128]{3,2,1,0:T(8,128)S(1)}, u32[]{:S(2)}, u32[]{:S(2)}) collective-permute-start(f32[2,4,32,128]{3,2,1,0:T(8,128)S(1)} %shard_map.101), channel_id=1, source_target_pairs={{0,3},{1,2},{2,1},{3,0},{4,7},{5,6},{6,5},{7,4},{8,11},{9,10},{10,... | collective-permute-start | bytes 393224 | tf_op jit(solution)/shard_map/ppermute | solution.py:574
  37.6 5.8 %collective-permute-start.13 = (f32[2,4,32,128]{3,2,1,0:T(8,128)S(1)}, f32[2,4,32,128]{3,2,1,0:T(8,128)S(1)}, u32[]{:S(2)}, u32[]{:S(2)}) collective-permute-start(f32[2,4,32,128]{3,2,1,0:T(8,128)S(1)} %shard_map.100), channel_id=1, source_target_pairs={{0,2},{1,3},{2,0},{3,1},{4,6},{5,7},{6,4},{7,5},{8,10},{9,11},{10,... | collective-permute-start | bytes 393224 | tf_op jit(solution)/shard_map/ppermute | solution.py:574
  39.4 5.0 %collective-permute-start.12 = (f32[2,4,32,128]{3,2,1,0:T(8,128)S(1)}, f32[2,4,32,128]{3,2,1,0:T(8,128)S(1)}, u32[]{:S(2)}, u32[]{:S(2)}) collective-permute-start(f32[2,4,32,128]{3,2,1,0:T(8,128)S(1)} %shard_map.99), channel_id=1, source_target_pairs={{0,1},{1,0},{2,3},{3,2},{4,5},{5,4},{6,7},{7,6},{8,9},{9,8},{10,11... | collective-permute-start | bytes 393224 | tf_op jit(solution)/shard_map/ppermute | solution.py:574
  40.2 4.2 %collective-permute-start.15 = (f32[2,4,32,128]{3,2,1,0:T(8,128)S(1)}, f32[2,4,32,128]{3,2,1,0:T(8,128)S(1)}, u32[]{:S(2)}, u32[]{:S(2)}) collective-permute-start(f32[2,4,32,128]{3,2,1,0:T(8,128)S(1)} %shard_map.98.refs_0_), channel_id=1, source_target_pairs={{0,16},{16,0},{1,17},{17,1},{2,18},{18,2},{3,19},{19,3},{4,20},{20... | collective-permute-start | bytes 393224 | tf_op jit(solution)/shard_map/ppermute | solution.py:570
  42.0 2.4 %collective-permute-start.18 = (f32[2,4,32,128]{3,2,1,0:T(8,128)S(1)}, f32[2,4,32,128]{3,2,1,0:T(8,128)S(1)}, u32[]{:S(2)}, u32[]{:S(2)}) collective-permute-start(f32[2,4,32,128]{3,2,1,0:T(8,128)S(1)} %collective-permute-done.14.refs_3_), channel_id=1, source_target_pairs={{0,16},{16,0},{1,17},{17,1},{2,18},{18,2},{3,19},{19,3},{4,20},{20... | collective-permute-start | bytes 393224 | tf_op jit(solution)/shard_map/ppermute | solution.py:570
  43.4 1.3 %collective-permute-start.17 = (f32[2,4,32,128]{3,2,1,0:T(8,128)S(1)}, f32[2,4,32,128]{3,2,1,0:T(8,128)S(1)}, u32[]{:S(2)}, u32[]{:S(2)}) collective-permute-start(f32[2,4,32,128]{3,2,1,0:T(8,128)S(1)} %collective-permute-done.13.refs_2_), channel_id=1, source_target_pairs={{0,16},{16,0},{1,17},{17,1},{2,18},{18,2},{3,19},{19,3},{4,20},{20... | collective-permute-start | bytes 393224 | tf_op jit(solution)/shard_map/ppermute | solution.py:570
  44.4 1.3 %collective-permute-start.16 = (f32[2,4,32,128]{3,2,1,0:T(8,128)S(1)}, f32[2,4,32,128]{3,2,1,0:T(8,128)S(1)}, u32[]{:S(2)}, u32[]{:S(2)}) collective-permute-start(f32[2,4,32,128]{3,2,1,0:T(8,128)S(1)} %collective-permute-done.12.refs_1_), channel_id=1, source_target_pairs={{0,16},{16,0},{1,17},{17,1},{2,18},{18,2},{3,19},{19,3},{4,20},{20... | collective-permute-start | bytes 393224 | tf_op jit(solution)/shard_map/ppermute | solution.py:570

commit v2 on v1

--- a/solution.py
+++ b/solution.py
@@ -12,7 +12,7 @@
 LOC = 4
 LANES = 128
 SUB = 8
-LEVELS_AT_ONCE = 4
+LEVELS_AT_ONCE = 8
 GROUP = ("section", "mem")
 F32 = jnp.float32
 BF16 = jnp.bfloat16
@@ -395,26 +395,42 @@
     return call(centre_kernel, outs, place, keep, other, *near, mean)
 
 
-def transform_kernel(fields, place_ref, part_ref, za_ref, zb_ref, a_ref, b_ref, weight_ref, *refs):
+def near_gram_kernel(fields, place_ref, part_ref, near_ref, info_ref, weight_ref, out_ref, *scratch):
+    read = info_reader(place_ref, info_ref, fields, True)
+    obs = near_ref.shape[3]
+    weight = weight_ref[:, obs : 2 * obs]
+    out_ref[...] = part_ref[...] + gram_of(place_ref, near_ref, read, weight, *scratch)
+
+
+def near_gram(place, part, near, info, weight, fields):
+    members, obs = ensemble(near)
+    return call(
+        functools.partial(near_gram_kernel, fields),
+        [(part.shape, F32)],
+        place,
+        part,
+        near,
+        info,
+        weight,
+        scratch=gram_scratch(members, obs),
+    )[0]
+
+
+def transform_kernel(fields, place_ref, part_ref, near_ref, info_ref, weight_ref, *refs):
     inv_ref, mean_ref, y_ref, zh_ref, zl_ref, gram_ref, low_ref, s_ref = refs
-    obs = y_ref.shape[1]
-    members = y_ref.shape[0]
+    members, obs = y_ref.shape
     starts, offsets, total = pair_rows(members)
-    sums = part_ref[...]
-    for n, (near_ref, info_ref) in enumerate(((za_ref, a_ref), (zb_ref, b_ref))):
-        read = info_reader(place_ref, info_ref, fields, n == 0)
-        weight = weight_ref[:, pl.ds((n + 1) * obs, obs)]
-        sums = sums + gram_of(place_ref, near_ref, read, weight, y_ref, zh_ref, zl_ref)
+    read = info_reader(place_ref, info_ref, fields, False)
+    weight = weight_ref[:, 2 * obs : 3 * obs]
+    sums = part_ref[...] + gram_of(place_ref, near_ref, read, weight, y_ref, zh_ref, zl_ref)
 
     width = sums.shape[1]
     domain = lax.broadcasted_iota(jnp.int32, (width, LANES), 0) % (width // 2)
     column = lax.broadcasted_iota(jnp.int32, (width, LANES), 1) // DB
     spread = (domain == column).astype(F32).astype(BF16)
     high, low = split_2(sums)
-    rest = (sums - high.astype(F32) - low.astype(F32)).astype(BF16)
     gram = jnp.dot(high, spread, preferred_element_type=F32)
     gram = gram + jnp.dot(low, spread, preferred_element_type=F32)
-    gram = gram + jnp.dot(rest, spread, preferred_element_type=F32)
     gram_ref[...] = gram
 
     sub_row = lax.broadcasted_iota(jnp.int32, (SUB, LANES), 0)
@@ -455,18 +471,16 @@
         mean_ref[pl.ds(b * SUB, SUB), :] = mean[b]
 
 
-def transforms(place, part, near_a, near_b, a, b, weight, fields):
-    members, obs = ensemble(near_a)
+def transforms(place, part, near, info, weight, fields):
+    members, obs = ensemble(near)
     _, _, total = pair_rows(members)
     return call(
         functools.partial(transform_kernel, fields),
         [((members, members, LANES), F32), ((members, LANES), F32)],
         place,
         part,
-        near_a,
-        near_b,
-        a,
-        b,
+        near,
+        info,
         weight,
         scratch=gram_scratch(members, obs)
         + [
@@ -605,7 +619,9 @@
     other_obs = to_partner(own_obs)
     other = to_partner(send)
     both_obs = jnp.stack([own_obs, other_obs])
-    gathered = [both_obs] + [over_mem(both_obs, k) for k in far[::-1]]
+    gathered = [both_obs]
+    for k in far[::-1]:
+        gathered.append(over_mem(both_obs, k))
     gathered = jnp.stack(gathered)
     joined = join(place, keep, other)
     near = []
@@ -614,7 +630,8 @@
     near_a, near_b = along_tile(gathered, gathered)
     weight = weights(place, lists, counts, info, a, b, memb_dev * levels)
     part = own_gram(place, gathered, info, weight)
-    inverse, mean = transforms(place, part, near_a, near_b, a, b, weight, memb_dev * levels)
+    part = near_gram(place, part, near_a, a, weight, memb_dev * levels)
+    inverse, mean = transforms(place, part, near_b, b, weight, memb_dev * levels)
     anomaly, base = centre(place, keep, other, near, mean)
 
     direct = None

time: 47.1 us -> 47 us (level)
    pallas_call x11 -> x12, Pallas kernels: 10.2 us -> 10.1 us  [call(): pl.pallas_call(lambda *refs: kernel(position(*place), *refs), in_specs=[v...]
where the time goes in v2:
time: 47 us; the launch traced here: 46.6 us
  starting transfers between devices  20.4 us (43%)
  waiting for transfers between devices  14 us (30%)
  Pallas kernels  11 us (23%)
  local copies, waits for them, and re-layouts  0.83 us (2%)
    ppermute x9, starting transfers between devices, over_mem(): lax.ppermute(value, 'mem', [(i, i ^ k) for i in range(lax.axis_size('mem'...  10.7 us
    pallas_call x12, Pallas kernels, call(): pl.pallas_call(lambda *refs: kernel(position(*place), *refs), in_specs=[v...  10.1 us
    ppermute x4, starting transfers between devices, trade(): return lax.ppermute(value, 'tile', pairs)  9.09 us
    ppermute x9, waiting for transfers between devices, over_mem(): lax.ppermute(value, 'mem', [(i, i ^ k) for i in range(lax.axis_size('mem'...  7.73 us
    ppermute x4, waiting for transfers between devices, trade(): return lax.ppermute(value, 'tile', pairs)  4.28 us
    ppermute x6, waiting for transfers between devices, to_partner(): return lax.ppermute(value, 'section', [(0, 1), (1, 0)])  2.02 us
  transfers between devices with their start and end apart: 19, of which 10 were waited for; matrix products, arithmetic and copies ran while one was open for 2% of the time, Pallas kernels for 12%

profile of v2, /device:TPU:0, one launch (start us, length us, event | category | flops | bytes accessed | tf_op | source)
XLA Modules:
  0.0 46.6 jit_solution(7049489435300849966)
XLA Ops:
  0.0 0.0 copy-start
  0.0 0.0 copy-start.1
  0.0 0.0 copy-start.2
  0.0 0.0 copy-start.3
  0.0 0.0 copy-start.4
  0.0 1.4 %shard_map.91 = (f32[97,4,128]{2,1,0:T(4,128)S(1)}, f32[97,4,128]{2,1,0:T(4,128)S(1)}, f32[32,128]{1,0:T(8,128)S(1)}) custom-call(f32[64,16,128]{2,1,0:T(8,128)} %bitcast.17, f32[16,16,128]{2,1,0:T(8,128)} %refs_3_.3, f32[16,16,128]{2,1,0:T(8,128)} %refs_4_.1, f32[16,128]{1,0:T(8,128)} %refs_5_.1, s32[8,128]{1,0:T(8,128)} %bitcast.19, f32[8,128]{1,0:T(8,128)} %bitcast.26, ...), custom_call_target="tpu_custom_call" | custom-call | tf_op jit(solution)/shard_map/pallas_call | solution.py:38
  1.4 0.0 copy-start.5
  1.4 3.1 %collective-permute-start = (f32[97,4,128]{2,1,0:T(4,128)S(1)}, f32[97,4,128]{2,1,0:T(4,128)S(1)}, u32[]{:S(2)}, u32[]{:S(2)}) collective-permute-start(f32[97,4,128]{2,1,0:T(4,128)S(1)} %get-tuple-element.18), channel_id=1, source_target_pairs={{0,4},{4,0},{8,12},{12,8},{1,5},{5,1},{9,13},{13,9},{2,6},{6,2},{1... | collective-permute-start | bytes 595976 | tf_op jit(solution)/shard_map/ppermute | solution.py:576
  4.5 0.7 %collective-permute-start.1 = (f32[97,4,128]{2,1,0:T(4,128)S(1)}, f32[97,4,128]{2,1,0:T(4,128)S(1)}, u32[]{:S(2)}, u32[]{:S(2)}) collective-permute-start(f32[97,4,128]{2,1,0:T(4,128)S(1)} %get-tuple-element.19), channel_id=1, source_target_pairs={{4,8},{8,4},{5,9},{9,5},{6,10},{10,6},{7,11},{11,7},{20,24},{24,20... | collective-permute-start | bytes 595976 | tf_op jit(solution)/shard_map/ppermute | solution.py:576
  5.2 4.3 %collective-permute-done.refs_1_.refs_3_.refs_2_ = f32[97,4,128]{2,1,0:T(4,128)S(1)} collective-permute-done((f32[97,4,128]{2,1,0:T(4,128)S(1)}, f32[97,4,128]{2,1,0:T(4,128)S(1)}, u32[]{:S(2)}, u32[]{:S(2)}) %collective-permute-start) | collective-permute-done | bytes 198688 | tf_op jit(solution)/shard_map/ppermute | solution.py:576
  9.5 0.0 collective-permute-done.1.refs_2_.refs_4_
  9.5 0.0 copy-done.1
  9.5 0.0 copy-done.2
  9.5 0.0 copy-done.3
  9.5 0.0 copy-done.4
  9.5 0.0 copy-done.5
  9.5 2.8 %shard_map.92 = (f32[4,4,32,128]{3,2,1,0:T(8,128)S(1)}, f32[4,4,32,128]{3,2,1,0:T(8,128)S(1)}, f32[4,1024]{1,0:T(4,128)S(1)}) custom-call(f32[64,16,128]{2,1,0:T(8,128)S(1)} %bitcast.18, f32[97,4,128]{2,1,0:T(4,128)S(1)} %collective-permute-done.refs_1_.refs_3_.refs_2_, f32[97,4,128]{2,1,0:T(4,128)S(1)} %collective-permute-done.1.refs_2_.refs_4_, ...), custom_call_target="tpu_custom_call" | custom-call | tf_op jit(solution)/shard_map/pallas_call | solution.py:38
  12.3 0.1 collective-permute-start.6
  12.4 0.5 %collective-permute-start.2 = (f32[4,4,32,128]{3,2,1,0:T(8,128)S(1)}, f32[4,4,32,128]{3,2,1,0:T(8,128)S(1)}, u32[]{:S(2)}, u32[]{:S(2)}) collective-permute-start(f32[4,4,32,128]{3,2,1,0:T(8,128)S(1)} %get-tuple-element.21), channel_id=1, source_target_pairs={{0,16},{16,0},{1,17},{17,1},{2,18},{18,2},{3,19},{19,3},{4,20},{20... | collective-permute-start | bytes 786440 | tf_op jit(solution)/shard_map/ppermute | solution.py:584
  12.9 0.7 %collective-permute-done.6 = f32[4,1024]{1,0:T(4,128)S(1)} collective-permute-done((f32[4,1024]{1,0:T(4,128)S(1)}, f32[4,1024]{1,0:T(4,128)S(1)}, u32[]{:S(2)}, u32[]{:S(2)}) %collective-permute-start.6) | collective-permute-done | bytes 16416 | tf_op jit(solution)/shard_map/ppermute | solution.py:584
  13.6 2.7 %collective-permute-start.9 = (f32[2,4,1024]{2,1,0:T(4,128)S(1)}, f32[2,4,1024]{2,1,0:T(4,128)S(1)}, u32[]{:S(2)}, u32[]{:S(2)}) collective-permute-start(f32[2,4,1024]{2,1,0:T(4,128)S(1)} %get-tuple-element.32), channel_id=1, source_target_pairs={{0,3},{1,2},{2,1},{3,0},{4,7},{5,6},{6,5},{7,4},{8,11},{9,10},{10,... | collective-permute-start | bytes 98312 | tf_op jit(solution)/shard_map/ppermute | solution.py:588
  16.2 0.5 %collective-permute-start.7 = (f32[2,4,1024]{2,1,0:T(4,128)S(1)}, f32[2,4,1024]{2,1,0:T(4,128)S(1)}, u32[]{:S(2)}, u32[]{:S(2)}) collective-permute-start(f32[2,4,1024]{2,1,0:T(4,128)S(1)} %get-tuple-element.32), channel_id=1, source_target_pairs={{0,1},{1,0},{2,3},{3,2},{4,5},{5,4},{6,7},{7,6},{8,9},{9,8},{10,11... | collective-permute-start | bytes 98312 | tf_op jit(solution)/shard_map/ppermute | solution.py:588
  16.8 0.3 collective-permute-start.8
  17.1 1.3 %collective-permute-done.9 = f32[2,4,1024]{2,1,0:T(4,128)S(1)} collective-permute-done((f32[2,4,1024]{2,1,0:T(4,128)S(1)}, f32[2,4,1024]{2,1,0:T(4,128)S(1)}, u32[]{:S(2)}, u32[]{:S(2)}) %collective-permute-start.9) | collective-permute-done | bytes 32800 | tf_op jit(solution)/shard_map/ppermute | solution.py:588
  18.4 1.7 %collective-permute-done.7 = f32[2,4,1024]{2,1,0:T(4,128)S(1)} collective-permute-done((f32[2,4,1024]{2,1,0:T(4,128)S(1)}, f32[2,4,1024]{2,1,0:T(4,128)S(1)}, u32[]{:S(2)}, u32[]{:S(2)}) %collective-permute-start.7) | collective-permute-done | bytes 32800 | tf_op jit(solution)/shard_map/ppermute | solution.py:588
  20.1 0.5 %collective-permute-done.8 = f32[2,4,1024]{2,1,0:T(4,128)S(1)} collective-permute-done((f32[2,4,1024]{2,1,0:T(4,128)S(1)}, f32[2,4,1024]{2,1,0:T(4,128)S(1)}, u32[]{:S(2)}, u32[]{:S(2)}) %collective-permute-start.8) | collective-permute-done | bytes 32800 | tf_op jit(solution)/shard_map/ppermute | solution.py:588
  20.7 4.7 %collective-permute-start.10 = (f32[4,2,4,1024]{3,2,1,0:T(4,128)S(1)}, f32[4,2,4,1024]{3,2,1,0:T(4,128)S(1)}, u32[]{:S(2)}, u32[]{:S(2)}) collective-permute-start(f32[4,2,4,1024]{3,2,1,0:T(4,128)S(1)} %pad_maximum_fusion.refs_0_), channel_id=1, source_target_pairs={{0,4},{4,0},{8,12},{12,8},{1,5},{5,1},{9,13},{13,9},{2,6},{6,2},{1... | collective-permute-start | bytes 393224 | tf_op jit(solution)/shard_map/ppermute | solution.py:576
  25.4 0.7 %collective-permute-start.11 = (f32[4,2,4,1024]{3,2,1,0:T(4,128)S(1)}, f32[4,2,4,1024]{3,2,1,0:T(4,128)S(1)}, u32[]{:S(2)}, u32[]{:S(2)}) collective-permute-start(f32[4,2,4,1024]{3,2,1,0:T(4,128)S(1)} %pad_maximum_fusion.refs_0_), channel_id=1, source_target_pairs={{4,8},{8,4},{5,9},{9,5},{6,10},{10,6},{7,11},{11,7},{20,24},{24,20... | collective-permute-start | bytes 393224 | tf_op jit(solution)/shard_map/ppermute | solution.py:576
  26.0 0.0 collective-permute-done.2.refs_1_
  26.1 1.6 %collective-permute-start.3 = (f32[2,4,32,128]{3,2,1,0:T(8,128)S(1)}, f32[2,4,32,128]{3,2,1,0:T(8,128)S(1)}, u32[]{:S(2)}, u32[]{:S(2)}) collective-permute-start(f32[2,4,32,128]{3,2,1,0:T(8,128)S(1)} %get-tuple-element.22), channel_id=1, source_target_pairs={{0,1},{1,0},{2,3},{3,2},{4,5},{5,4},{6,7},{7,6},{8,9},{9,8},{10,11... | collective-permute-start | bytes 393224 | tf_op jit(solution)/shard_map/ppermute | solution.py:588
  27.6 0.5 %collective-permute-start.4 = (f32[2,4,32,128]{3,2,1,0:T(8,128)S(1)}, f32[2,4,32,128]{3,2,1,0:T(8,128)S(1)}, u32[]{:S(2)}, u32[]{:S(2)}) collective-permute-start(f32[2,4,32,128]{3,2,1,0:T(8,128)S(1)} %get-tuple-element.23), channel_id=1, source_target_pairs={{0,2},{1,3},{2,0},{3,1},{4,6},{5,7},{6,4},{7,5},{8,10},{9,11},{10,... | collective-permute-start | bytes 393224 | tf_op jit(solution)/shard_map/ppermute | solution.py:588
  28.1 1.5 %collective-permute-start.5 = (f32[2,4,32,128]{3,2,1,0:T(8,128)S(1)}, f32[2,4,32,128]{3,2,1,0:T(8,128)S(1)}, u32[]{:S(2)}, u32[]{:S(2)}) collective-permute-start(f32[2,4,32,128]{3,2,1,0:T(8,128)S(1)} %get-tuple-element.24), channel_id=1, source_target_pairs={{0,3},{1,2},{2,1},{3,0},{4,7},{5,6},{6,5},{7,4},{8,11},{9,10},{10,... | collective-permute-start | bytes 393224 | tf_op jit(solution)/shard_map/ppermute | solution.py:588
  29.6 0.7 %dynamic-slice_bitcast_fusion.1 = s32[64,1]{0,1:T(1,128)S(1)} fusion(s32[8,64]{1,0:T(8,128)} %param.17, s32[]{:T(128)S(6)} %select_n.4), kind=kLoop, calls=%fused_computation.3 | loop fusion | bytes 516 | tf_op jit(solution)/shard_map/reshape | solution.py:611
  30.3 0.1 copy.10.refs_1_
  30.4 0.0 copy-done
  30.5 0.9 %shard_map.94.refs_2_.refs_3_ = bf16[128,3072]{1,0:T(8,128)(2,1)S(1)} custom-call(s32[64,256]{1,0:T(8,128)S(1)} %dynamic-slice_bitcast_fusion.refs_0_, s32[64,1]{1,0:T(8,128)S(1)} %copy.10.refs_1_, f32[32,128]{1,0:T(8,128)S(1)} %get-tuple-element.26.refs_2_.refs_1_, f32[97,4,128]{2,1,0:T(4,128)S(1)} %collective-permute-done.refs_1_.refs_3_.refs_2_, ...), custom_call_target="tpu_custom_call" | custom-call | tf_op jit(solution)/shard_map/pallas_call | solution.py:38
  31.3 0.9 %shard_map.95.refs_0_ = f32[672,128]{1,0:T(8,128)S(1)} custom-call(f32[4,2,4,1024]{3,2,1,0:T(4,128)S(1)} %pad_maximum_fusion.refs_0_, f32[32,128]{1,0:T(8,128)S(1)} %get-tuple-element.26.refs_2_.refs_1_, bf16[128,3072]{1,0:T(8,128)(2,1)S(1)} %shard_map.94.refs_2_.refs_3_), custom_call_target="tpu_custom_call" | custom-call | tf_op jit(solution)/shard_map/pallas_call | solution.py:38
  32.2 0.0 collective-permute-done.10.refs_1_
  32.3 1.0 %shard_map.96.refs_0_ = f32[672,128]{1,0:T(8,128)S(1)} custom-call(f32[672,128]{1,0:T(8,128)S(1)} %shard_map.95.refs_0_, f32[4,2,4,1024]{3,2,1,0:T(4,128)S(1)} %collective-permute-done.10.refs_1_, f32[97,4,128]{2,1,0:T(4,128)S(1)} %collective-permute-done.refs_1_.refs_3_.refs_2_, bf16[128,3072]{1,0:T(8,128)(2,1)S(1)} %shard_map.94.refs_2_.refs_3_), custom_call_target="tpu_custom_call" | custom-call | tf_op jit(solution)/shard_map/pallas_call | solution.py:38
  33.3 0.0 collective-permute-done.11.refs_1_
  33.3 2.1 %shard_map.97 = (f32[32,32,128]{2,1,0:T(8,128)S(1)}, f32[32,128]{1,0:T(8,128)S(1)}) custom-call(f32[672,128]{1,0:T(8,128)S(1)} %shard_map.96.refs_0_, f32[4,2,4,1024]{3,2,1,0:T(4,128)S(1)} %collective-permute-done.11.refs_1_, f32[97,4,128]{2,1,0:T(4,128)S(1)} %collective-permute-done.1.refs_2_.refs_4_, bf16[128,3072]{1,0:T(8,128)(2,1)S(1)} %shard_map.94.refs_2_.refs_3_), custom_call_target="tpu_custom_call" | custom-call | tf_op jit(solution)/shard_map/pallas_call | solution.py:38
  35.4 0.0 collective-permute-done.3.refs_2_
  35.4 0.0 collective-permute-done.4.refs_3_
  35.4 0.0 collective-permute-done.5.refs_4_
  35.4 0.2 shard_map.98
  35.6 0.3 shard_map.102
  35.9 1.4 %collective-permute-start.14 = (f32[2,4,32,128]{3,2,1,0:T(8,128)S(1)}, f32[2,4,32,128]{3,2,1,0:T(8,128)S(1)}, u32[]{:S(2)}, u32[]{:S(2)}) collective-permute-start(f32[2,4,32,128]{3,2,1,0:T(8,128)S(1)} %shard_map.102), channel_id=1, source_target_pairs={{0,3},{1,2},{2,1},{3,0},{4,7},{5,6},{6,5},{7,4},{8,11},{9,10},{10,... | collective-permute-start | bytes 393224 | tf_op jit(solution)/shard_map/ppermute | solution.py:588
  37.3 0.2 shard_map.101
  37.5 1.6 %collective-permute-start.13 = (f32[2,4,32,128]{3,2,1,0:T(8,128)S(1)}, f32[2,4,32,128]{3,2,1,0:T(8,128)S(1)}, u32[]{:S(2)}, u32[]{:S(2)}) collective-permute-start(f32[2,4,32,128]{3,2,1,0:T(8,128)S(1)} %shard_map.101), channel_id=1, source_target_pairs={{0,2},{1,3},{2,0},{3,1},{4,6},{5,7},{6,4},{7,5},{8,10},{9,11},{10,... | collective-permute-start | bytes 393224 | tf_op jit(solution)/shard_map/ppermute | solution.py:588
  39.1 0.2 shard_map.100
  39.3 0.6 %collective-permute-start.12 = (f32[2,4,32,128]{3,2,1,0:T(8,128)S(1)}, f32[2,4,32,128]{3,2,1,0:T(8,128)S(1)}, u32[]{:S(2)}, u32[]{:S(2)}) collective-permute-start(f32[2,4,32,128]{3,2,1,0:T(8,128)S(1)} %shard_map.100), channel_id=1, source_target_pairs={{0,1},{1,0},{2,3},{3,2},{4,5},{5,4},{6,7},{7,6},{8,9},{9,8},{10,11... | collective-permute-start | bytes 393224 | tf_op jit(solution)/shard_map/ppermute | solution.py:588
  40.0 0.2 shard_map.99.refs_0_
  40.1 0.1 collective-permute-start.15
  40.2 1.8 %collective-permute-done.14.refs_3_ = f32[2,4,32,128]{3,2,1,0:T(8,128)S(1)} collective-permute-done((f32[2,4,32,128]{3,2,1,0:T(8,128)S(1)}, f32[2,4,32,128]{3,2,1,0:T(8,128)S(1)}, u32[]{:S(2)}, u32[]{:S(2)}) %collective-permute-start.14) | collective-permute-done | bytes 131104 | tf_op jit(solution)/shard_map/ppermute | solution.py:588
  42.0 0.0 collective-permute-start.18
  42.0 1.3 %collective-permute-done.13.refs_2_ = f32[2,4,32,128]{3,2,1,0:T(8,128)S(1)} collective-permute-done((f32[2,4,32,128]{3,2,1,0:T(8,128)S(1)}, f32[2,4,32,128]{3,2,1,0:T(8,128)S(1)}, u32[]{:S(2)}, u32[]{:S(2)}) %collective-permute-start.13) | collective-permute-done | bytes 131104 | tf_op jit(solution)/shard_map/ppermute | solution.py:588
  43.3 0.0 collective-permute-start.17
  43.3 1.0 %collective-permute-done.12.refs_1_ = f32[2,4,32,128]{3,2,1,0:T(8,128)S(1)} collective-permute-done((f32[2,4,32,128]{3,2,1,0:T(8,128)S(1)}, f32[2,4,32,128]{3,2,1,0:T(8,128)S(1)}, u32[]{:S(2)}, u32[]{:S(2)}) %collective-permute-start.12) | collective-permute-done | bytes 131104 | tf_op jit(solution)/shard_map/ppermute | solution.py:588
  44.4 0.0 collective-permute-start.16
  44.4 0.0 collective-permute-done.15.refs_4_
  44.4 0.0 collective-permute-done.18.refs_7_
  44.4 0.3 collective-permute-done.17.refs_6_
  44.7 1.0 %collective-permute-done.16.refs_5_ = f32[2,4,32,128]{3,2,1,0:T(8,128)S(1)} collective-permute-done((f32[2,4,32,128]{3,2,1,0:T(8,128)S(1)}, f32[2,4,32,128]{3,2,1,0:T(8,128)S(1)}, u32[]{:S(2)}, u32[]{:S(2)}) %collective-permute-start.16) | collective-permute-done | bytes 131104 | tf_op jit(solution)/shard_map/ppermute | solution.py:584
  45.7 0.9 %unpack.1 = f32[4,256,128]{2,1,0:T(8,128)} custom-call(f32[2,4,32,128]{3,2,1,0:T(8,128)S(1)} %shard_map.99.refs_0_, f32[2,4,32,128]{3,2,1,0:T(8,128)S(1)} %collective-permute-done.12.refs_1_, f32[2,4,32,128]{3,2,1,0:T(8,128)S(1)} %collective-permute-done.13.refs_2_, f32[2,4,32,128]{3,2,1,0:T(8,128)S(1)} %collective-permute-done.14.refs_3_, ...), custom_call_target="tpu_custom_call" | custom-call | tf_op jit(solution)/shard_map/unpack/pallas_call | solution.py:558
  (4 shorter events, 0.1 us)
Async XLA Ops:
  0.0 30.4 %copy-start = (s32[8,64,256]{2,1,0:T(8,128)S(1)}, s32[8,64,256]{2,1,0:T(8,128)}, u32[]{:S(2)}) copy-start(s32[8,64,256]{2,1,0:T(8,128)} %param.16) | copy-start | bytes 1572868
  0.0 9.5 %copy-start.1 = (f32[4,16,16,128]{3,2,1,0:T(8,128)S(1)}, f32[4,16,16,128]{3,2,1,0:T(8,128)}, u32[]{:S(2)}) copy-start(f32[4,16,16,128]{3,2,1,0:T(8,128)} %param.9) | copy-start | bytes 1572868
  0.0 9.5 %copy-start.2 = (f32[16,16,128]{2,1,0:T(8,128)S(1)}, f32[16,16,128]{2,1,0:T(8,128)}, u32[]{:S(2)}) copy-start(f32[16,16,128]{2,1,0:T(8,128)} %refs_3_.3) | copy-start | bytes 393220
  0.0 9.5 %copy-start.3 = (f32[16,16,128]{2,1,0:T(8,128)S(1)}, f32[16,16,128]{2,1,0:T(8,128)}, u32[]{:S(2)}) copy-start(f32[16,16,128]{2,1,0:T(8,128)} %refs_4_.1) | copy-start | bytes 393220
  0.0 9.5 %copy-start.4 = (f32[16,128]{1,0:T(8,128)S(1)}, f32[16,128]{1,0:T(8,128)}, u32[]{:S(2)}) copy-start(f32[16,128]{1,0:T(8,128)} %refs_5_.1) | copy-start | bytes 24580
  1.4 8.1 %copy-start.5 = (s32[1024]{0:T(1024)S(1)}, s32[1024]{0:T(1024)}, u32[]{:S(2)}) copy-start(s32[1024]{0:T(1024)} %param.13) | copy-start | bytes 12292
  1.4 8.1 %collective-permute-start = (f32[97,4,128]{2,1,0:T(4,128)S(1)}, f32[97,4,128]{2,1,0:T(4,128)S(1)}, u32[]{:S(2)}, u32[]{:S(2)}) collective-permute-start(f32[97,4,128]{2,1,0:T(4,128)S(1)} %get-tuple-element.18), channel_id=1, source_target_pairs={{0,4},{4,0},{8,12},{12,8},{1,5},{5,1},{9,13},{13,9},{2,6},{6,2},{1... | collective-permute-start | bytes 595976 | tf_op jit(solution)/shard_map/ppermute | solution.py:576
  4.5 4.9 %collective-permute-start.1 = (f32[97,4,128]{2,1,0:T(4,128)S(1)}, f32[97,4,128]{2,1,0:T(4,128)S(1)}, u32[]{:S(2)}, u32[]{:S(2)}) collective-permute-start(f32[97,4,128]{2,1,0:T(4,128)S(1)} %get-tuple-element.19), channel_id=1, source_target_pairs={{4,8},{8,4},{5,9},{9,5},{6,10},{10,6},{7,11},{11,7},{20,24},{24,20... | collective-permute-start | bytes 595976 | tf_op jit(solution)/shard_map/ppermute | solution.py:576
  12.3 1.2 %collective-permute-start.6 = (f32[4,1024]{1,0:T(4,128)S(1)}, f32[4,1024]{1,0:T(4,128)S(1)}, u32[]{:S(2)}, u32[]{:S(2)}) collective-permute-start(f32[4,1024]{1,0:T(4,128)S(1)} %get-tuple-element.25), channel_id=1, source_target_pairs={{0,16},{16,0},{1,17},{17,1},{2,18},{18,2},{3,19},{19,3},{4,20},{20... | collective-permute-start | bytes 49160 | tf_op jit(solution)/shard_map/ppermute | solution.py:584
  12.4 13.7 %collective-permute-start.2 = (f32[4,4,32,128]{3,2,1,0:T(8,128)S(1)}, f32[4,4,32,128]{3,2,1,0:T(8,128)S(1)}, u32[]{:S(2)}, u32[]{:S(2)}) collective-permute-start(f32[4,4,32,128]{3,2,1,0:T(8,128)S(1)} %get-tuple-element.21), channel_id=1, source_target_pairs={{0,16},{16,0},{1,17},{17,1},{2,18},{18,2},{3,19},{19,3},{4,20},{20... | collective-permute-start | bytes 786440 | tf_op jit(solution)/shard_map/ppermute | solution.py:584
  13.6 4.9 %collective-permute-start.9 = (f32[2,4,1024]{2,1,0:T(4,128)S(1)}, f32[2,4,1024]{2,1,0:T(4,128)S(1)}, u32[]{:S(2)}, u32[]{:S(2)}) collective-permute-start(f32[2,4,1024]{2,1,0:T(4,128)S(1)} %get-tuple-element.32), channel_id=1, source_target_pairs={{0,3},{1,2},{2,1},{3,0},{4,7},{5,6},{6,5},{7,4},{8,11},{9,10},{10,... | collective-permute-start | bytes 98312 | tf_op jit(solution)/shard_map/ppermute | solution.py:588
  16.2 3.9 %collective-permute-start.7 = (f32[2,4,1024]{2,1,0:T(4,128)S(1)}, f32[2,4,1024]{2,1,0:T(4,128)S(1)}, u32[]{:S(2)}, u32[]{:S(2)}) collective-permute-start(f32[2,4,1024]{2,1,0:T(4,128)S(1)} %get-tuple-element.32), channel_id=1, source_target_pairs={{0,1},{1,0},{2,3},{3,2},{4,5},{5,4},{6,7},{7,6},{8,9},{9,8},{10,11... | collective-permute-start | bytes 98312 | tf_op jit(solution)/shard_map/ppermute | solution.py:588
  16.8 3.9 %collective-permute-start.8 = (f32[2,4,1024]{2,1,0:T(4,128)S(1)}, f32[2,4,1024]{2,1,0:T(4,128)S(1)}, u32[]{:S(2)}, u32[]{:S(2)}) collective-permute-start(f32[2,4,1024]{2,1,0:T(4,128)S(1)} %get-tuple-element.32), channel_id=1, source_target_pairs={{0,2},{1,3},{2,0},{3,1},{4,6},{5,7},{6,4},{7,5},{8,10},{9,11},{10,... | collective-permute-start | bytes 98312 | tf_op jit(solution)/shard_map/ppermute | solution.py:588
  20.7 11.5 %collective-permute-start.10 = (f32[4,2,4,1024]{3,2,1,0:T(4,128)S(1)}, f32[4,2,4,1024]{3,2,1,0:T(4,128)S(1)}, u32[]{:S(2)}, u32[]{:S(2)}) collective-permute-start(f32[4,2,4,1024]{3,2,1,0:T(4,128)S(1)} %pad_maximum_fusion.refs_0_), channel_id=1, source_target_pairs={{0,4},{4,0},{8,12},{12,8},{1,5},{5,1},{9,13},{13,9},{2,6},{6,2},{1... | collective-permute-start | bytes 393224 | tf_op jit(solution)/shard_map/ppermute | solution.py:576
  25.4 7.9 %collective-permute-start.11 = (f32[4,2,4,1024]{3,2,1,0:T(4,128)S(1)}, f32[4,2,4,1024]{3,2,1,0:T(4,128)S(1)}, u32[]{:S(2)}, u32[]{:S(2)}) collective-permute-start(f32[4,2,4,1024]{3,2,1,0:T(4,128)S(1)} %pad_maximum_fusion.refs_0_), channel_id=1, source_target_pairs={{4,8},{8,4},{5,9},{9,5},{6,10},{10,6},{7,11},{11,7},{20,24},{24,20... | collective-permute-start | bytes 393224 | tf_op jit(solution)/shard_map/ppermute | solution.py:576
  26.1 9.3 %collective-permute-start.3 = (f32[2,4,32,128]{3,2,1,0:T(8,128)S(1)}, f32[2,4,32,128]{3,2,1,0:T(8,128)S(1)}, u32[]{:S(2)}, u32[]{:S(2)}) collective-permute-start(f32[2,4,32,128]{3,2,1,0:T(8,128)S(1)} %get-tuple-element.22), channel_id=1, source_target_pairs={{0,1},{1,0},{2,3},{3,2},{4,5},{5,4},{6,7},{7,6},{8,9},{9,8},{10,11... | collective-permute-start | bytes 393224 | tf_op jit(solution)/shard_map/ppermute | solution.py:588
  27.6 7.8 %collective-permute-start.4 = (f32[2,4,32,128]{3,2,1,0:T(8,128)S(1)}, f32[2,4,32,128]{3,2,1,0:T(8,128)S(1)}, u32[]{:S(2)}, u32[]{:S(2)}) collective-permute-start(f32[2,4,32,128]{3,2,1,0:T(8,128)S(1)} %get-tuple-element.23), channel_id=1, source_target_pairs={{0,2},{1,3},{2,0},{3,1},{4,6},{5,7},{6,4},{7,5},{8,10},{9,11},{10,... | collective-permute-start | bytes 393224 | tf_op jit(solution)/shard_map/ppermute | solution.py:588
  28.1 7.3 %collective-permute-start.5 = (f32[2,4,32,128]{3,2,1,0:T(8,128)S(1)}, f32[2,4,32,128]{3,2,1,0:T(8,128)S(1)}, u32[]{:S(2)}, u32[]{:S(2)}) collective-permute-start(f32[2,4,32,128]{3,2,1,0:T(8,128)S(1)} %get-tuple-element.24), channel_id=1, source_target_pairs={{0,3},{1,2},{2,1},{3,0},{4,7},{5,6},{6,5},{7,4},{8,11},{9,10},{10,... | collective-permute-start | bytes 393224 | tf_op jit(solution)/shard_map/ppermute | solution.py:588
  35.9 6.1 %collective-permute-start.14 = (f32[2,4,32,128]{3,2,1,0:T(8,128)S(1)}, f32[2,4,32,128]{3,2,1,0:T(8,128)S(1)}, u32[]{:S(2)}, u32[]{:S(2)}) collective-permute-start(f32[2,4,32,128]{3,2,1,0:T(8,128)S(1)} %shard_map.102), channel_id=1, source_target_pairs={{0,3},{1,2},{2,1},{3,0},{4,7},{5,6},{6,5},{7,4},{8,11},{9,10},{10,... | collective-permute-start | bytes 393224 | tf_op jit(solution)/shard_map/ppermute | solution.py:588
  37.5 5.8 %collective-permute-start.13 = (f32[2,4,32,128]{3,2,1,0:T(8,128)S(1)}, f32[2,4,32,128]{3,2,1,0:T(8,128)S(1)}, u32[]{:S(2)}, u32[]{:S(2)}) collective-permute-start(f32[2,4,32,128]{3,2,1,0:T(8,128)S(1)} %shard_map.101), channel_id=1, source_target_pairs={{0,2},{1,3},{2,0},{3,1},{4,6},{5,7},{6,4},{7,5},{8,10},{9,11},{10,... | collective-permute-start | bytes 393224 | tf_op jit(solution)/shard_map/ppermute | solution.py:588
  39.3 5.0 %collective-permute-start.12 = (f32[2,4,32,128]{3,2,1,0:T(8,128)S(1)}, f32[2,4,32,128]{3,2,1,0:T(8,128)S(1)}, u32[]{:S(2)}, u32[]{:S(2)}) collective-permute-start(f32[2,4,32,128]{3,2,1,0:T(8,128)S(1)} %shard_map.100), channel_id=1, source_target_pairs={{0,1},{1,0},{2,3},{3,2},{4,5},{5,4},{6,7},{7,6},{8,9},{9,8},{10,11... | collective-permute-start | bytes 393224 | tf_op jit(solution)/shard_map/ppermute | solution.py:588
  40.1 4.2 %collective-permute-start.15 = (f32[2,4,32,128]{3,2,1,0:T(8,128)S(1)}, f32[2,4,32,128]{3,2,1,0:T(8,128)S(1)}, u32[]{:S(2)}, u32[]{:S(2)}) collective-permute-start(f32[2,4,32,128]{3,2,1,0:T(8,128)S(1)} %shard_map.99.refs_0_), channel_id=1, source_target_pairs={{0,16},{16,0},{1,17},{17,1},{2,18},{18,2},{3,19},{19,3},{4,20},{20... | collective-permute-start | bytes 393224 | tf_op jit(solution)/shard_map/ppermute | solution.py:584
  42.0 2.4 %collective-permute-start.18 = (f32[2,4,32,128]{3,2,1,0:T(8,128)S(1)}, f32[2,4,32,128]{3,2,1,0:T(8,128)S(1)}, u32[]{:S(2)}, u32[]{:S(2)}) collective-permute-start(f32[2,4,32,128]{3,2,1,0:T(8,128)S(1)} %collective-permute-done.14.refs_3_), channel_id=1, source_target_pairs={{0,16},{16,0},{1,17},{17,1},{2,18},{18,2},{3,19},{19,3},{4,20},{20... | collective-permute-start | bytes 393224 | tf_op jit(solution)/shard_map/ppermute | solution.py:584
  43.3 1.3 %collective-permute-start.17 = (f32[2,4,32,128]{3,2,1,0:T(8,128)S(1)}, f32[2,4,32,128]{3,2,1,0:T(8,128)S(1)}, u32[]{:S(2)}, u32[]{:S(2)}) collective-permute-start(f32[2,4,32,128]{3,2,1,0:T(8,128)S(1)} %collective-permute-done.13.refs_2_), channel_id=1, source_target_pairs={{0,16},{16,0},{1,17},{17,1},{2,18},{18,2},{3,19},{19,3},{4,20},{20... | collective-permute-start | bytes 393224 | tf_op jit(solution)/shard_map/ppermute | solution.py:584
  44.4 1.3 %collective-permute-start.16 = (f32[2,4,32,128]{3,2,1,0:T(8,128)S(1)}, f32[2,4,32,128]{3,2,1,0:T(8,128)S(1)}, u32[]{:S(2)}, u32[]{:S(2)}) collective-permute-start(f32[2,4,32,128]{3,2,1,0:T(8,128)S(1)} %collective-permute-done.12.refs_1_), channel_id=1, source_target_pairs={{0,16},{16,0},{1,17},{17,1},{2,18},{18,2},{3,19},{19,3},{4,20},{20... | collective-permute-start | bytes 393224 | tf_op jit(solution)/shard_map/ppermute | solution.py:584
